TPU v7x, 32 devices: a whole 2x2x4 slice. The times are simulated.
32 devices in a mesh: cfg: 2 (over core), seq: 8 (over z, x), tile: 2 (over y).
Axes of the slice: x: 2, y: 2, z: 4, core: 2. Of those that a mesh axis runs over, the one named last changes fastest.
Arguments:
- section_input: bfloat16 [4, 128, 64, 384], P('tile', None, 'seq'), may hold values from -6 to 6
- norm_gain: float32 [384], replicated, may hold values from 0.5 to 1.5
- conv_weight: bfloat16 [384, 864], replicated, may hold values from -0.0625 to 0.0625
- conv_bias: float32 [32], replicated, may hold values from -3 to 3
- mean_weight: float32 [32, 16], replicated, may hold values from -1 to 1
- mean_bias: float32 [16], replicated, may hold values from -3 to 3
- noisy_tokens: bfloat16 [8192, 64], P(('seq', 'tile')), may hold values from -6 to 6
- mask_tokens: bfloat16 [8192, 128], P(('seq', 'tile')), may hold values from 0 to 1
- patch_weight: bfloat16 [64, 5120], replicated, may hold values from -0.75 to 0.75
- patch_bias: float32 [5120], replicated, may hold values from -3 to 3
- context_weight: bfloat16 [192, 5120], replicated, may hold values from -0.4375 to 0.4375
- context_bias: float32 [5120], replicated, may hold values from -3 to 3
- norm_shift: float32 [5120], replicated, may hold values from -3 to 3
- norm_scale: float32 [5120], replicated, may hold values from -3 to 3
Outputs:
- block_input: bfloat16 [8192, 5120], P(('seq', 'tile'))
All inputs are finite; a program needn't handle non-finite values.
Results may differ from a plain program's by a relative error of at most 0.004.
Values may be sent and summed in bfloat16 or wider, within the bound.
A program may use at most 128 MiB of HBM per device.

v0:
```python
import functools

import jax
import jax.numpy as jnp
from jax import lax
from jax.experimental import pallas as pl
from jax.experimental.pallas import tpu as pltpu
from jax.sharding import PartitionSpec as P

K = 3
MESH = pl.DeviceIdType.MESH
F32 = jnp.float32
BF16 = jnp.bfloat16


def ones_where(shape, test):
    i = lax.broadcasted_iota(jnp.int32, shape, 0)
    j = lax.broadcasted_iota(jnp.int32, shape, 1)
    return jnp.where(test(i, j), 1.0, 0.0)


def nt(x, y):
    return lax.dot_general(x, y, (((1,), (1,)), ((), ())), preferred_element_type=F32)


def fold_weights(cw_ref, mw_ref, wt):
    z, zo = mw_ref.shape
    mw = mw_ref[...]
    high = mw.astype(BF16)
    low = (mw - high.astype(F32)).astype(BF16)
    spread = ones_where((4 * z, z), lambda i, j: i % z == j).astype(BF16)
    copier = ones_where((zo, K * zo), lambda i, j: j % zo == i).astype(BF16)

    def right_slot(i, j):
        slot, e = i // z, j // zo
        return ((slot == 0) & (e == 1)) | ((slot == 2) & (e == 0)) | ((slot == 3) & (e == 2))

    keep = ones_where((4 * z, K * zo), right_slot)
    parts = []
    for part in (high, low):
        tall = jnp.dot(spread, part, preferred_element_type=F32).astype(BF16)
        parts.append((jnp.dot(tall, copier, preferred_element_type=F32) * keep).astype(BF16))
    parts = jnp.concatenate(parts, axis=0)
    nothing = jnp.zeros((z, wt.shape[2]), BF16)
    for a in range(K):
        for b in range(K):
            at = (a * K + b) * K * zo
            rhs = cw_ref[at : at + K * zo, :]
            res = jnp.dot(parts, rhs, preferred_element_type=F32)
            res = (res[: 4 * z] + res[4 * z :]).astype(BF16)
            for f in range(2):
                for slot in range(4):
                    row = slot * 4 * z + (f + 2 - a) * z
                    wt[f * K + b, row : row + z, :] = res[slot * z : (slot + 1) * z]
    for b in range(K):
        for slot in range(4):
            row = slot * 4 * z
            wt[b, row + 3 * z : row + 4 * z, :] = nothing
            wt[K + b, row : row + z, :] = nothing


def fold_bias(mw_ref, cb_ref, mb_ref):
    z = mw_ref.shape[0]
    copier = ones_where((128, z), lambda i, j: i % z == j)
    exact = functools.partial(
        lax.dot_general, dimension_numbers=(((1,), (1,)), ((), ())),
        precision=lax.Precision.HIGHEST, preferred_element_type=F32,
    )
    return exact(exact(cb_ref[...], mw_ref[...]) + mb_ref[...], copier)


def head_kernel(
    sizes, x_hbm, cw_ref, gain_ref, mw_ref, cb_ref, mb_ref, out_ref,
    wt, xin, actf, acc, edge, pk, rs_send, ls_send, ca_send, rs_got, ls_got, ca_got, patch,
    in_sem, s1_sem, r1_sem, s2_sem, r2_sem,
):
    n_c, n_s, n_t, shard_rows = sizes
    c, s, t = lax.axis_index("cfg"), lax.axis_index("seq"), lax.axis_index("tile")
    frames, height, columns, channels = x_hbm.shape
    half = height // n_c
    pairs = half // 2
    z = 16
    chunks = pairs // shard_rows
    chunk_tokens = shard_rows * (columns // 2)

    def dev(ci, si, ti):
        return {"cfg": ci, "seq": si, "tile": ti}

    load = pltpu.make_async_copy(
        x_hbm.at[:, pl.ds(c * (half - 1), half + 1)],
        xin.at[:, pl.ds(1 - c, half + 1)],
        in_sem,
    )
    load.start()

    barrier = pltpu.get_barrier_semaphore()
    links = [(1, 0), (-1, 0), (0, 1), (1, 1), (-1, 1)]

    def there(ds, dt, sign):
        si, ti = s + sign * ds, t + sign * dt
        return (si >= 0) & (si < n_s) & (ti >= 0) & (ti < n_t), si, ti

    expect = jnp.int32(0)
    for ds, dt in links:
        ok, si, ti = there(ds, dt, -1)

        @pl.when(ok)
        def _():
            pl.semaphore_signal(barrier, inc=1, device_id=dev(c, si, ti), device_id_type=MESH)

        ok, _, _ = there(ds, dt, 1)
        expect = expect + ok.astype(jnp.int32)

    first = (s * n_t + t) * shard_rows
    src_t = first // (height // 2) // frames
    src_c = first % (height // 2) // pairs
    for si in range(n_s):
        mine = (src_c == c) & (src_t == t) & (s == si)

        @pl.when(jnp.logical_not(mine))
        def _():
            pl.semaphore_signal(barrier, inc=1, device_id=dev(src_c, si, src_t), device_id_type=MESH)

    own = (src_c == c) & (src_t == t)
    expect = expect + frames * chunks * n_c - own.astype(jnp.int32)

    fold_weights(cw_ref, mw_ref, wt)
    bias = fold_bias(mw_ref, cb_ref, mb_ref)

    zero_row = jnp.zeros((frames, 1, columns, channels), BF16)

    @pl.when(c == 0)
    def _():
        xin[:, 0:1] = zero_row

    @pl.when(c == n_c - 1)
    def _():
        xin[:, half + 1 : half + 2] = zero_row

    load.wait()
    gain = gain_ref[...].reshape(1, channels)
    step_rows = 6 if (half + 2) % 6 == 0 else 2
    for f in range(frames):

        @pl.loop(0, (half + 2) // step_rows)
        def _(r):
            v = xin[f, pl.ds(r * step_rows, step_rows)].astype(F32)
            v = v.reshape(step_rows * columns, channels)
            energy = jnp.sum(v * v, axis=-1, keepdims=True) * (1.0 / channels)
            v = v * lax.rsqrt(energy + 1e-06) * gain
            v = v / (1.0 + jnp.exp(-v))
            at = pl.multiple_of(r * (step_rows * columns), step_rows * columns)
            actf[f, pl.ds(at, step_rows * columns), :] = v

    rows = half * columns
    for m in range(2):
        lo = m * (rows // 2)
        total = None
        for f in range(frames):
            for b in range(K):
                lhs = actf[f, lo + b * columns : lo + b * columns + rows // 2, :].astype(BF16)
                term = nt(lhs, wt[f * K + b])
                total = term if total is None else total + term
        acc[lo : lo + rows // 2, :] = total[:, :128]
        edge[lo : lo + rows // 2, :] = total[:, 128:]

    q = edge[...]
    w_at = lax.broadcasted_iota(jnp.int32, (rows, 128), 0) % columns
    right = jnp.where(w_at == 0, 0.0, pltpu.roll(q, 1, 0))
    left = jnp.where(w_at == columns - 1, 0.0, pltpu.roll(q, rows - 1, 0))
    acc[...] = acc[...] + right + pltpu.roll(left, 64, 1)
    rs_send[...] = edge[pl.ds(columns - 1, half, stride=columns), :].astype(BF16)
    ls_send[...] = edge[pl.ds(0, half, stride=columns), :].astype(BF16)
    quarter = rows // 4
    lane = lax.broadcasted_iota(jnp.int32, (quarter, 128), 1)
    packed = jnp.zeros((quarter, 128), F32)
    for k in range(4):
        part = pltpu.roll(acc[k * quarter : (k + 1) * quarter, :], (k * 32 + 128 - 32) % 128, 1)
        packed = jnp.where(lane // 32 == k, part, packed)
    ca_send[...] = packed.astype(BF16)

    pl.semaphore_wait(barrier, expect)

    bufs = {1: (rs_send, rs_got), -1: (ls_send, ls_got), 0: (ca_send, ca_got)}

    def link_copy(i, sign):
        ds, dt = links[i]
        ok, si, ti = there(ds, dt, sign)
        src, dst = bufs[ds]
        if ds != 0:
            dst = dst.at[dt]
        return ok, pltpu.make_async_remote_copy(
            src_ref=src, dst_ref=dst, send_sem=s1_sem.at[i], recv_sem=r1_sem.at[i],
            device_id=dev(c, si, ti), device_id_type=MESH,
        )

    for i in (2, 3, 4, 0, 1):
        ok, copy = link_copy(i, 1)

        @pl.when(ok)
        def _():
            copy.start()

    for i in (0, 1, 3, 4, 2):
        ds, dt = links[i]
        ok, copy = link_copy(i, -1)

        @pl.when(ok)
        def _():
            copy.wait_recv()
            if ds == 0:
                got = ca_got[...].astype(F32)
                for k in range(4):
                    acc[k * quarter : (k + 1) * quarter, :] += pltpu.roll(got, (128 - 32 * k) % 128, 1)
            else:
                got = bufs[ds][1][dt].astype(F32)
                turn = (128 - 32 * dt - (64 if ds < 0 else 0)) % 128
                if turn:
                    got = pltpu.roll(got, turn, 1)
                at = pl.ds(0 if ds > 0 else columns - 1, half, stride=columns)
                acc[at, :] = acc[at, :] + got

    total = acc[...] + bias
    by_row = total.reshape(pairs, 2, columns, 128)
    even = by_row[:, 0].reshape(pairs * columns, 128)
    odd = by_row[:, 1].reshape(pairs * columns, 128)
    lane = lax.broadcasted_iota(jnp.int32, (pairs * columns, 128), 1)
    mixed = jnp.where(
        lane < 16, even,
        jnp.where(
            lane < 32, pltpu.roll(odd, 16, 1),
            jnp.where(lane < 48, pltpu.roll(even, 16, 1), pltpu.roll(odd, 32, 1)),
        ),
    )
    pk[...] = mixed
    tokens = pairs * columns // 2
    left_half = pk[pl.ds(0, tokens, stride=2), :]
    right_half = pk[pl.ds(1, tokens, stride=2), :]
    lane = lax.broadcasted_iota(jnp.int32, (tokens, 128), 1)
    for f in range(frames):
        one = left_half if f == 0 else pltpu.roll(left_half, 128 - 32 * f, 1)
        two = pltpu.roll(right_half, (32 - 32 * f) % 128, 1) if f != 1 else right_half
        both = jnp.where(lane < 32, one, two)
        for m in range(chunks):
            patch[f * chunks + m] = both[m * chunk_tokens : (m + 1) * chunk_tokens, :64].astype(BF16)

    def patch_copy(f, m, ci):
        shard = ((t * frames + f) * (height // 2) + c * pairs) // shard_rows + m
        si, ti = shard // n_t, shard % n_t
        mine = (si == s) & (ti == t) & (c == ci)
        piece = f * chunks + m
        local = pltpu.make_async_copy(patch.at[piece], out_ref.at[s], r2_sem.at[s])
        away = pltpu.make_async_remote_copy(
            src_ref=patch.at[piece], dst_ref=out_ref.at[s],
            send_sem=s2_sem.at[piece * n_c + ci], recv_sem=r2_sem.at[s],
            device_id=dev(ci, si, ti), device_id_type=MESH,
        )
        return mine, local, away

    every = [(f, m, ci) for f in range(frames) for m in range(chunks) for ci in range(n_c)]
    for item in every:
        mine, local, away = patch_copy(*item)

        @pl.when(mine)
        def _():
            local.start()

        @pl.when(jnp.logical_not(mine))
        def _():
            away.start()

    for si in range(n_s):
        pltpu.make_async_copy(patch.at[0], out_ref.at[si], r2_sem.at[si]).wait()
    for i in range(5):
        ok, copy = link_copy(i, 1)

        @pl.when(ok)
        def _():
            copy.wait_send()

    for item in every:
        mine, _, away = patch_copy(*item)

        @pl.when(jnp.logical_not(mine))
        def _():
            away.wait_send()


def tail_kernel(noisy, mask, lat, pw, cw, pb, cb, shift, scale, out, comb, both, inv_ref, mean_ref, sems):
    split = lat.shape[-1]
    width = comb.shape[1]
    step = 512
    z = split // 4

    @pl.when(pl.program_id(0) == 0)
    def _():
        upper = pltpu.make_async_copy(pw, both.at[:split], sems.at[0])
        lower = pltpu.make_async_copy(cw, both.at[split:], sems.at[1])
        upper.start()
        lower.start()
        upper.wait()
        lower.wait()

    parts = comb.shape[0] // out.shape[0]

    @pl.when(pl.program_id(0) % parts == 0)
    def _():
        perm = ones_where(
            (split, split), lambda i, j: j == (i % z) * 4 + (i // z % 2) * 2 + i // (2 * z)
        ).astype(BF16)
        if len(lat.shape) == 3:
            strips, per, _ = lat.shape
            tokens = lat[...].reshape(strips * per, split)
            n, cols = strips * per, 4
            order = ones_where(
                (n, n),
                lambda i, j: j == (i // cols % strips) * per + i // (cols * strips) * cols + i % cols,
            ).astype(BF16)
            tokens = jnp.dot(order, tokens, preferred_element_type=F32).astype(BF16)
        else:
            tokens = lat[...]
        tokens = jnp.dot(tokens, perm, preferred_element_type=F32)
        own = noisy[...].astype(F32).T
        lhs = jnp.concatenate([own, tokens, mask[...].astype(F32)], axis=1).astype(BF16)
        total = None
        for k in range(0, width, step):
            at = slice(k, k + step)
            part = jnp.dot(lhs, both[:, at], preferred_element_type=F32)
            part = part + (pb[:, at] + cb[:, at])
            comb[:, at] = part
            term = jnp.sum(part, axis=-1, keepdims=True)
            total = term if total is None else total + term
        mean = total * (1.0 / width)
        square = None
        for k in range(0, width, step):
            d = comb[:, k : k + step] - mean
            term = jnp.sum(d * d, axis=-1, keepdims=True)
            square = term if square is None else square + term
        mean_ref[...] = jnp.broadcast_to(mean, mean_ref.shape)
        inv_ref[...] = jnp.broadcast_to(lax.rsqrt(square * (1.0 / width) + 1e-06), inv_ref.shape)

    rows = out.shape[0]
    mine = pl.ds(pl.multiple_of(pl.program_id(0) % parts * rows, rows), rows)
    mean, inv = mean_ref[mine, :1], inv_ref[mine, :1]
    for k in range(0, width, step):
        at = slice(k, k + step)
        out[:, at] = ((comb[mine, at] - mean) * inv * (1.0 + scale[:, at]) + shift[:, at]).astype(BF16)


def body(
    section_input, norm_gain, conv_weight, conv_bias, mean_weight, mean_bias, noisy_tokens,
    mask_tokens, patch_weight, patch_bias, context_weight, context_bias, norm_shift, norm_scale,
):
    frames, height, columns, channels = section_input.shape
    n_c, n_s, n_t = lax.axis_size("cfg"), lax.axis_size("seq"), lax.axis_size("tile")
    z = mean_weight.shape[1]
    tokens = noisy_tokens.shape[0]
    shard_rows = tokens // (n_s * columns // 2)
    half = height // n_c
    rows = half * columns
    chunks = half // 2 // shard_rows
    chunk_tokens = shard_rows * (columns // 2)
    vmem = pl.BlockSpec(memory_space=pltpu.VMEM)
    arrived = pl.pallas_call(
        functools.partial(head_kernel, (n_c, n_s, n_t, shard_rows)),
        out_shape=jax.ShapeDtypeStruct((n_s, chunk_tokens, 4 * z), BF16),
        in_specs=[pl.BlockSpec(memory_space=pltpu.HBM)] + [vmem] * 5,
        out_specs=vmem,
        scratch_shapes=[
            pltpu.VMEM((frames * K, 16 * z, channels), BF16),
            pltpu.VMEM((frames, half + 2, columns, channels), BF16),
            pltpu.VMEM((frames, (half + 2) * columns, channels), F32),
            pltpu.VMEM((rows, 128), F32),
            pltpu.VMEM((rows, 128), F32),
            pltpu.VMEM((rows // 2, 128), F32),
            pltpu.VMEM((half, 128), BF16),
            pltpu.VMEM((half, 128), BF16),
            pltpu.VMEM((rows // 4, 128), BF16),
            pltpu.VMEM((2, half, 128), BF16),
            pltpu.VMEM((2, half, 128), BF16),
            pltpu.VMEM((rows // 4, 128), BF16),
            pltpu.VMEM((frames * chunks, chunk_tokens, 4 * z), BF16),
            pltpu.SemaphoreType.DMA,
            pltpu.SemaphoreType.DMA((5,)),
            pltpu.SemaphoreType.DMA((5,)),
            pltpu.SemaphoreType.DMA((frames * chunks * n_c,)),
            pltpu.SemaphoreType.DMA((n_s,)),
        ],
        compiler_params=pltpu.CompilerParams(collective_id=0, has_side_effects=True),
        name="head",
    )(
        section_input, conv_weight.T, norm_gain, mean_weight.T, conv_bias[None], mean_bias[None]
    )
    width = patch_weight.shape[1]
    block = min(tokens, 256)
    per = block // n_s
    if per % 16 == 0 and columns == 8:
        lat = arrived
        lat_spec = pl.BlockSpec((n_s, per, 4 * z), lambda i: (0, i // parts, 0))
    else:
        lat = arrived.reshape(n_s, shard_rows, columns // 2, 4 * z).transpose(1, 0, 2, 3)
        lat = lat.reshape(tokens, 4 * z)
        lat_spec = pl.BlockSpec((block, 4 * z), lambda i: (i // parts, 0))
    parts = 2 if block % 32 == 0 else 1
    tok = lambda n: pl.BlockSpec((block, n), lambda i: (i // parts, 0))
    full = lambda a: pl.BlockSpec(a.shape, lambda i: (0, 0))
    hbm = pl.BlockSpec(memory_space=pl.ANY)
    depth = patch_weight.shape[0] + context_weight.shape[0]
    vecs = [v[None] for v in (patch_bias, context_bias, norm_shift, norm_scale)]
    return pl.pallas_call(
        tail_kernel,
        out_shape=jax.ShapeDtypeStruct((tokens, width), BF16),
        grid=(tokens // block * parts,),
        in_specs=[
            pl.BlockSpec((noisy_tokens.shape[1], block), lambda i: (0, i // parts)),
            tok(mask_tokens.shape[1]), lat_spec, hbm, hbm,
        ]
        + [full(v) for v in vecs],
        out_specs=pl.BlockSpec((block // parts, width), lambda i: (i, 0)),
        scratch_shapes=[
            pltpu.VMEM((block, width), F32),
            pltpu.VMEM((depth, width), BF16),
            pltpu.VMEM((block, 128), F32),
            pltpu.VMEM((block, 128), F32),
            pltpu.SemaphoreType.DMA((2,)),
        ],
        name="tail",
    )(noisy_tokens.T, mask_tokens, lat, patch_weight, context_weight, *vecs)


def solution(mesh):
    placed = (P("tile", None, "seq", None),) + (P(),) * 5
    placed = placed + (P(("seq", "tile"), None),) * 2 + (P(),) * 6
    return jax.shard_map(
        body, mesh=mesh, in_specs=placed, out_specs=P(("seq", "tile"), None), check_vma=False
    )
```

profile of v0, /device:TPU:0, one launch (start us, length us, event | category | flops | bytes accessed | tf_op | source)
XLA Modules:
  0.0 29.4 jit_solution(1773321439932648634)
XLA Ops:
  0.0 19.2 %head.1.lat = bf16[8,64,64]{2,1,0:T(8,128)(2,1)} custom-call(bf16[2,128,8,384]{3,2,1,0:T(8,128)(2,1)} %x_hbm.1, bf16[864,384]{1,0:T(8,128)(2,1)} %bitcast.9, f32[384]{0:T(512)} %gain_ref.1, f32[16,32]{1,0:T(8,128)} %bitcast.15, f32[1,32]{1,0:T(1,128)} %bitcast.16, f32[1,16]{1,0:T(1,128)} %bitcast.17), custom_call_target="tpu_custom_call" | custom-call | tf_op jit(solution)/shard_map/head/pallas_call | solution.py:364
  19.2 10.3 %tail.1 = bf16[512,5120]{1,0:T(8,128)(2,1)} custom-call(bf16[64,512]{1,0:T(8,128)(2,1)} %bitcast.10, bf16[512,128]{1,0:T(8,128)(2,1)} %mask.1, bf16[8,64,64]{2,1,0:T(8,128)(2,1)} %head.1.lat, bf16[64,5120]{1,0:T(8,128)(2,1)} %pw.1, bf16[192,5120]{1,0:T(8,128)(2,1)} %cw.1, f32[1,5120]{1,0:T(1,128)} %bitcast.11, f32[1,5120]{1,0:T(1,128)} %bitcast.12, ...), custom_call_target="tpu_custom_call" | custom-call | tf_op jit(solution)/shard_map/tail/pallas_call | solution.py:410
where the time goes:
time: 29.8 us; the launch traced here: 29.4 us
  Pallas kernels  29.4 us (99%)
    pallas_call x1, Pallas kernels, body(): pl.pallas_call(functools.partial(head_kernel, (n_c, n_s, n_t, shard_rows)...  19.2 us
    pallas_call x1, Pallas kernels, body(): pl.pallas_call(tail_kernel, out_shape=jax.ShapeDtypeStruct((tokens, width...  10.3 us

commit v1 on v0

--- a/solution.py
+++ b/solution.py
@@ -428,9 +428,403 @@
     )(noisy_tokens.T, mask_tokens, lat, patch_weight, context_weight, *vecs)
 
 
+def exact_nt(x, y):
+    return lax.dot_general(
+        x, y, (((1,), (1,)), ((), ())), precision=lax.Precision.HIGHEST, preferred_element_type=F32
+    )
+
+
+def halves(v):
+    high = v.astype(BF16)
+    return high, (v - high.astype(F32)).astype(BF16)
+
+
+def send_kernel(
+    sizes, x_hbm, cw_hbm, gain_ref, mw_ref, cb_ref, mb_ref, noisy_hbm, mask_hbm, pw_hbm, xw_hbm, pb_ref, xb_ref,
+    lhs_ref, both_ref, bias_ref, mean_ref, inv_ref,
+    cwt, wt, xin, actf, cen, edge, msg, got, lat_w, own, mask, gram, rows, stack, lanes, in_sem, s_sem, r_sem,
+):
+    n_c, n_s, n_t, shard_rows = sizes
+    c, s, t = lax.axis_index("cfg"), lax.axis_index("seq"), lax.axis_index("tile")
+    frames, height, columns, channels = x_hbm.shape
+    half = height // n_c
+    pairs = half // 2
+    z = mw_ref.shape[0]
+    chunks = pairs // shard_rows
+    reach = frames + K - 1
+    split = 4 * z
+    width = both_ref.shape[1]
+
+    def dev(ci, si, ti):
+        return {"cfg": ci, "seq": si, "tile": ti}
+
+    loads = [
+        pltpu.make_async_copy(
+            x_hbm.at[f, pl.ds(c * (half - 1), half + 1)],
+            xin.at[f, pl.ds(1 - c, half + 1)],
+            in_sem.at[f],
+        )
+        for f in range(frames)
+    ]
+    for load in loads:
+        load.start()
+    taps = pltpu.make_async_copy(cw_hbm, cwt, in_sem.at[frames])
+    taps.start()
+    later = [
+        pltpu.make_async_copy(noisy_hbm, own, in_sem.at[frames + 1]),
+        pltpu.make_async_copy(mask_hbm, mask, in_sem.at[frames + 2]),
+        pltpu.make_async_copy(xw_hbm.at[:split], lat_w, in_sem.at[frames + 3]),
+        pltpu.make_async_copy(pw_hbm, both_ref.at[:split], in_sem.at[frames + 4]),
+        pltpu.make_async_copy(xw_hbm.at[split:], both_ref.at[2 * split :], in_sem.at[frames + 5]),
+    ]
+
+    barrier = pltpu.get_barrier_semaphore()
+    first = (s * n_t + t) * shard_rows
+    frame = first // (height // 2)
+    src_t = frame // frames
+    src_c = first % (height // 2) // pairs
+    carried = (src_t > 0) & (frame % frames < K - 1)
+    for si in range(n_s):
+        for back in range(2):
+            mine = (src_c == c) & (src_t - back == t) & (s == si)
+            wanted = jnp.logical_not(mine)
+            if back:
+                wanted = wanted & carried
+
+            @pl.when(wanted)
+            def _():
+                pl.semaphore_signal(
+                    barrier, inc=1, device_id=dev(src_c, si, src_t - back), device_id_type=MESH
+                )
+
+    def piece(g, m, ci):
+        at = t * frames + g
+        shard = (at * (height // 2) + c * pairs) // shard_rows + m
+        si, ti = shard // n_t, shard % n_t
+        mine = (si == s) & (ti == t) & (c == ci)
+        valid = at < n_t * frames
+        return mine, valid, si, ti
+
+    every = [(g, m, ci) for g in range(reach) for m in range(chunks) for ci in range(n_c)]
+    expect = jnp.int32(0)
+    for item in every:
+        mine, valid, _, _ = piece(*item)
+        expect = expect + (valid & jnp.logical_not(mine)).astype(jnp.int32)
+
+    zero_row = jnp.zeros((frames, 1, columns, channels), BF16)
+
+    @pl.when(c == 0)
+    def _():
+        xin[:, 0:1] = zero_row
+
+    @pl.when(c == n_c - 1)
+    def _():
+        xin[:, half + 1 : half + 2] = zero_row
+
+    taps.wait()
+    with jax.named_scope("fold"):
+        fold_weights(cwt, mw_ref, wt)
+        bias = fold_bias(mw_ref, cb_ref, mb_ref)
+
+    for load in loads:
+        load.wait()
+    for load in later:
+        load.start()
+    gain = gain_ref[...].reshape(1, channels)
+    step_rows = 6 if (half + 2) % 6 == 0 else 2
+    with jax.named_scope("act"):
+        for f in range(frames):
+
+            @pl.loop(0, (half + 2) // step_rows)
+            def _(r):
+                v = xin[f, pl.ds(r * step_rows, step_rows)].astype(F32)
+                v = v.reshape(step_rows * columns, channels)
+                energy = jnp.sum(v * v, axis=-1, keepdims=True) * (1.0 / channels)
+                v = v * lax.rsqrt(energy + 1e-06) * gain
+                v = v / (1.0 + jnp.exp(-v))
+                at = pl.multiple_of(r * (step_rows * columns), step_rows * columns)
+                actf[f, pl.ds(at, step_rows * columns), :] = v
+
+    count = half * columns
+    with jax.named_scope("conv"):
+        for m in range(2):
+            lo = m * (count // 2)
+            total = None
+            for f in range(frames):
+                for b in range(K):
+                    lhs = actf[f, lo + b * columns : lo + b * columns + count // 2, :].astype(BF16)
+                    term = nt(lhs, wt[f * K + b])
+                    total = term if total is None else total + term
+            cen[lo : lo + count // 2, :] = total[:, :128]
+            edge[lo : lo + count // 2, :] = total[:, 128:]
+
+    with jax.named_scope("pack"):
+        lane = lax.broadcasted_iota(jnp.int32, (8, 128), 1)
+        upper = lane >= 64
+        one = lane // z % 2 == 1
+        two = lane // z % 4 >= 2
+        for m in range(chunks):
+            cols = {}
+            for a in range(2):
+                mids, rights, lefts = [], [], []
+                for w in range(columns):
+                    starts = [((m * shard_rows + h * 8) * 2 + a) * columns + w for h in range(2)]
+                    c0, c1 = (cen[pl.ds(at, 8, stride=2 * columns), :] for at in starts)
+                    e0, e1 = (edge[pl.ds(at, 8, stride=2 * columns), :] for at in starts)
+                    mids.append(jnp.where(upper, pltpu.roll(c1, 64, 1), c0))
+                    turned = pltpu.roll(jnp.where(upper, e0, e1), 64, 1)
+                    rights.append(jnp.where(upper, turned, e0))
+                    lefts.append(jnp.where(upper, e1, turned))
+                for w in range(columns):
+                    v = mids[w]
+                    if w > 0:
+                        v = v + rights[w - 1]
+                    if w < columns - 1:
+                        v = v + lefts[w + 1]
+                    cols[a, w] = v
+                cols[a, columns] = rights[columns - 1]
+                cols[a, columns + 1] = lefts[0]
+            for j in range(columns // 2 + 1):
+                p = [cols[a, 2 * j + b] for b in range(2) for a in range(2)]
+                q = [None] * 4
+                for k in (0, 2):
+                    q[k] = jnp.where(one, pltpu.roll(p[k + 1], z, 1), p[k])
+                    q[k + 1] = jnp.where(one, p[k + 1], pltpu.roll(p[k], 128 - z, 1))
+                for k in range(2):
+                    low = jnp.where(two, pltpu.roll(q[k + 2], 2 * z, 1), q[k])
+                    high = jnp.where(two, q[k + 2], pltpu.roll(q[k], 128 - 2 * z, 1))
+                    msg[k * chunks + m, j * 8 : j * 8 + 8, :] = low.astype(BF16)
+                    msg[(k + 2) * chunks + m, j * 8 : j * 8 + 8, :] = high.astype(BF16)
+
+    with jax.named_scope("barrierwait"):
+        pl.semaphore_wait(barrier, expect)
+
+    def piece_copy(g, m, ci):
+        mine, valid, si, ti = piece(g, m, ci)
+        slot = g // frames
+        src, dst = msg.at[g * chunks + m], got.at[slot, s]
+        local = pltpu.make_async_copy(src, dst, r_sem.at[slot, s])
+        away = pltpu.make_async_remote_copy(
+            src_ref=src, dst_ref=dst, send_sem=s_sem.at[(g * chunks + m) * n_c + ci],
+            recv_sem=r_sem.at[slot, s], device_id=dev(ci, si, ti), device_id_type=MESH,
+        )
+        return mine & valid, jnp.logical_not(mine) & valid, local, away
+
+    with jax.named_scope("send"):
+        for item in every:
+            here, there, local, away = piece_copy(*item)
+
+            @pl.when(here)
+            def _():
+                local.start()
+
+            @pl.when(there)
+            def _():
+                away.start()
+
+    with jax.named_scope("prep"):
+        b = pb_ref[...] + xb_ref[...]
+        b = b - jnp.sum(b, axis=-1, keepdims=True) * (1.0 / width)
+        bias_ref[...] = b
+        for load in later:
+            load.wait()
+        swap = ones_where(
+            (split, split), lambda i, j: j == (i % z) * 4 + (i // z % 2) * 2 + i // (2 * z)
+        ).astype(BF16)
+        step = 512
+        for k in range(0, width, step):
+            part = jnp.dot(swap, lat_w[:, k : k + step], preferred_element_type=F32)
+            both_ref[split : 2 * split, k : k + step] = part.astype(BF16)
+        high, rest = b.astype(BF16), None
+        rest = b - high.astype(F32)
+        mid = rest.astype(BF16)
+        low = (rest - mid.astype(F32)).astype(BF16)
+        row = lax.broadcasted_iota(jnp.int32, (8, width), 0)
+        rows[...] = jnp.where(
+            row == 0, 1.0,
+            jnp.where(row == 1, high.astype(F32), jnp.where(row == 2, mid.astype(F32), jnp.where(row == 3, low.astype(F32), 0.0))),
+        ).astype(BF16)
+        energy = jnp.sum(b * b, axis=-1, keepdims=True)
+        square = nt(both_ref[...], both_ref[...])
+        high, low = halves(square)
+        gram[0] = high
+        gram[1] = low
+        sums = nt(rows[...], both_ref[...])
+        wmean = sums[0:1] * (1.0 / width)
+        cross = (sums[1:2] + sums[2:3] + sums[3:4]) * 2.0
+        noise = own[...].astype(F32).T
+        lanes[...] = jnp.concatenate([noise, noise], axis=1)
+        lhs_ref[:, 2 * split :] = mask[...]
+
+    per = columns // 2 * 8
+    with jax.named_scope("recv"):
+        for si in range(n_s):
+            pltpu.make_async_copy(msg.at[0], got.at[0, si], r_sem.at[0, si]).wait()
+
+        @pl.when(carried)
+        def _():
+            for si in range(n_s):
+                pltpu.make_async_copy(msg.at[0], got.at[1, si], r_sem.at[1, si]).wait()
+
+    with jax.named_scope("assemble"):
+        lane = lax.broadcasted_iota(jnp.int32, (8, 128), 1)
+        odd = lane // (2 * z) % 2 == 1
+
+        def strip(slot, si):
+            v = got[slot, si, :per, :].astype(F32)
+            parts = [v[k : k + 8] for k in range(0, per, 8)]
+            if si > 0:
+                parts[0] = parts[0] + jnp.where(odd, 0.0, got[slot, si - 1, per:, :].astype(F32))
+            if si < n_s - 1:
+                parts[-1] = parts[-1] + jnp.where(odd, got[slot, si + 1, per:, :].astype(F32), 0.0)
+            return jnp.concatenate(parts, axis=0)
+
+        for si in range(n_s):
+            stack[si * per : (si + 1) * per, :] = strip(0, si) + bias
+
+        @pl.when(carried)
+        def _():
+            for si in range(n_s):
+                at = slice(si * per, (si + 1) * per)
+                stack[at, :] = stack[at, :] + strip(1, si)
+
+        n = n_s * per
+        cols = columns // 2
+        order = ones_where(
+            (n, n), lambda i, j: j == (i // cols % n_s) * per + i % cols * 8 + i // (cols * n_s)
+        ).astype(BF16)
+        tokens = jnp.dot(order, stack[...].astype(BF16), preferred_element_type=F32)
+        lane = lax.broadcasted_iota(jnp.int32, (n, 128), 1)
+        for h in range(2):
+            mine = pltpu.roll(tokens, 64, 1) if h == 0 else tokens
+            at = slice(h * n, (h + 1) * n)
+            lhs_ref[at, : 2 * split] = jnp.where(lane < 64, lanes[at, :], mine).astype(BF16)
+
+    with jax.named_scope("stats"):
+        block = 128
+        for k in range(0, lhs_ref.shape[0], block):
+            at = slice(k, k + block)
+            x = lhs_ref[at, :]
+            y = jnp.dot(x, gram[0], preferred_element_type=F32) + jnp.dot(x, gram[1], preferred_element_type=F32)
+            x = x.astype(F32)
+            mean = jnp.sum(x * wmean, axis=-1, keepdims=True)
+            power = jnp.sum(x * (y + cross), axis=-1, keepdims=True) + energy
+            variance = jnp.maximum(power * (1.0 / width) - mean * mean, 0.0)
+            mean_ref[at, :] = jnp.broadcast_to(mean, (block, 128))
+            inv_ref[at, :] = jnp.broadcast_to(lax.rsqrt(variance + 1e-06), (block, 128))
+
+    with jax.named_scope("drain"):
+        for item in every:
+            _, there, _, away = piece_copy(*item)
+
+            @pl.when(there)
+            def _():
+                away.wait_send()
+
+
+def write_kernel(lhs, both, bias, mean, inv, shift, scale, out):
+    tokens, wide = out.shape
+    step = min(512, wide)
+    block = 128
+    for k in range(0, wide, step):
+        at = slice(k, k + step)
+        gain, add, move = 1.0 + scale[:, at], bias[:, at], shift[:, at]
+        for r in range(0, tokens, block):
+            rows = slice(r, r + block)
+            part = jnp.dot(lhs[rows, :], both[:, at], preferred_element_type=F32)
+            out[rows, at] = (((part + add) - mean[rows, :1]) * inv[rows, :1] * gain + move).astype(BF16)
+
+
+def fast(
+    section_input, norm_gain, conv_weight, conv_bias, mean_weight, mean_bias, noisy_tokens,
+    mask_tokens, patch_weight, patch_bias, context_weight, context_bias, norm_shift, norm_scale,
+):
+    frames, height, columns, channels = section_input.shape
+    n_c, n_s, n_t = lax.axis_size("cfg"), lax.axis_size("seq"), lax.axis_size("tile")
+    z = mean_weight.shape[1]
+    tokens, width = noisy_tokens.shape[0], patch_weight.shape[1]
+    shard_rows = tokens // (n_s * columns // 2)
+    half = height // n_c
+    count = half * columns
+    chunks = half // 2 // shard_rows
+    reach = frames + K - 1
+    per = (columns // 2 + 1) * 8
+    depth = patch_weight.shape[0] + context_weight.shape[0]
+    split = 4 * z
+    vmem = pl.BlockSpec(memory_space=pltpu.VMEM)
+    hbm = pl.BlockSpec(memory_space=pltpu.HBM)
+    n = n_s * columns // 2 * 8
+    prepared = pl.pallas_call(
+        functools.partial(send_kernel, (n_c, n_s, n_t, shard_rows)),
+        out_shape=(
+            pltpu.VMEM((tokens, depth), BF16),
+            pltpu.VMEM((depth, width), BF16),
+            pltpu.VMEM((1, width), F32),
+            pltpu.VMEM((tokens, 128), F32),
+            pltpu.VMEM((tokens, 128), F32),
+        ),
+        in_specs=[hbm, hbm] + [vmem] * 4 + [hbm] * 4 + [vmem] * 2,
+        out_specs=(vmem,) * 5,
+        scratch_shapes=[
+            pltpu.VMEM(conv_weight.shape[::-1], BF16),
+            pltpu.VMEM((frames * K, 16 * z, channels), BF16),
+            pltpu.VMEM((frames, half + 2, columns, channels), BF16),
+            pltpu.VMEM((frames, (half + 2) * columns, channels), F32),
+            pltpu.VMEM((count, 128), F32),
+            pltpu.VMEM((count, 128), F32),
+            pltpu.VMEM((reach * chunks, per, 128), BF16),
+            pltpu.VMEM((2, n_s, per, 128), BF16),
+            pltpu.VMEM((split, width), BF16),
+            pltpu.VMEM(noisy_tokens.shape[::-1], BF16),
+            pltpu.VMEM(mask_tokens.shape, BF16),
+            pltpu.VMEM((2, depth, depth), BF16),
+            pltpu.VMEM((8, width), BF16),
+            pltpu.VMEM((n, 128), F32),
+            pltpu.VMEM((tokens, 128), F32),
+            pltpu.SemaphoreType.DMA((frames + 6,)),
+            pltpu.SemaphoreType.DMA((reach * chunks * n_c,)),
+            pltpu.SemaphoreType.DMA((2, n_s)),
+        ],
+        compiler_params=pltpu.CompilerParams(
+            collective_id=0, has_side_effects=True, vmem_limit_bytes=40 * 2**20
+        ),
+        name="send",
+    )(
+        *(
+            pltpu.with_memory_space_constraint(v, pltpu.HBM)
+            for v in (
+                section_input, conv_weight.T, norm_gain, mean_weight.T, conv_bias[None], mean_bias[None],
+                noisy_tokens.T, mask_tokens, patch_weight, context_weight, patch_bias[None], context_bias[None],
+            )
+        )
+    )
+    wide = width // 5 if width % (5 * 512) == 0 else width
+    col = lambda r: pl.BlockSpec((r, wide), lambda i: (0, i))
+    full = lambda a: pl.BlockSpec(a.shape, lambda i: (0, 0))
+    lhs, both, bias, mean, inv = prepared
+    return pl.pallas_call(
+        write_kernel,
+        out_shape=jax.ShapeDtypeStruct((tokens, width), BF16),
+        grid=(width // wide,),
+        in_specs=[full(lhs), col(depth), col(1), full(mean), full(inv), col(1), col(1)],
+        out_specs=col(tokens),
+        compiler_params=pltpu.CompilerParams(vmem_limit_bytes=24 * 2**20),
+        name="write",
+    )(*prepared, norm_shift[None], norm_scale[None])
+
+
+def choose(*args):
+    n_c, n_s, n_t = lax.axis_size("cfg"), lax.axis_size("seq"), lax.axis_size("tile")
+    frames, height, columns, _ = args[0].shape
+    rows = args[6].shape[0] // (n_s * columns // 2)
+    fits = columns == 8 and args[4].shape[1] == 16 and frames == 2 and rows == 16
+    fits = fits and height // n_c // 2 % rows == 0
+    return fast(*args) if fits else body(*args)
+
+
 def solution(mesh):
     placed = (P("tile", None, "seq", None),) + (P(),) * 5
     placed = placed + (P(("seq", "tile"), None),) * 2 + (P(),) * 6
     return jax.shard_map(
-        body, mesh=mesh, in_specs=placed, out_specs=P(("seq", "tile"), None), check_vma=False
+        choose, mesh=mesh, in_specs=placed, out_specs=P(("seq", "tile"), None), check_vma=False
     )

time: 29.8 us -> 21.3 us (0.71)
  Pallas kernels: 29.4 us -> 21.1 us
    pallas_call x2, Pallas kernels: 29.4 us -> 21.1 us  [the longest x1 16 us: fast(): pl.pallas_call(functools.partial(send_kernel, (n_c, n_s, n_t, shard_rows)...]
where the time goes in v1:
time: 21.3 us; the launch traced here: 21.1 us
  Pallas kernels  21.1 us (99%)
    pallas_call x1, Pallas kernels, fast(): pl.pallas_call(functools.partial(send_kernel, (n_c, n_s, n_t, shard_rows)...  16 us
    pallas_call x1, Pallas kernels, fast(): pl.pallas_call(write_kernel, out_shape=jax.ShapeDtypeStruct((tokens, widt...  5.04 us

profile of v1, /device:TPU:0, one launch (start us, length us, event | category | flops | bytes accessed | tf_op | source)
XLA Modules:
  0.0 21.1 jit_solution(16120593121966796474)
XLA Ops:
  0.0 0.0 copy-start.1
  0.0 0.0 copy-start
  0.0 16.0 %send.1 = (bf16[512,256]{1,0:T(8,128)(2,1)S(1)}, bf16[256,5120]{1,0:T(8,128)(2,1)S(1)}, f32[1,5120]{1,0:T(1,128)S(1)}, f32[512,128]{1,0:T(8,128)S(1)}, f32[512,128]{1,0:T(8,128)S(1)}) custom-call(bf16[2,128,8,384]{3,2,1,0:T(8,128)(2,1)} %x_hbm.1, bf16[864,384]{1,0:T(8,128)(2,1)} %bitcast.11, f32[384]{0:T(512)} %gain_ref.1, f32[16,32]{1,0:T(8,128)} %bitcast.15, ...), custom_call_target="tpu_custom_call" | custom-call | tf_op jit(solution)/shard_map/send/pallas_call | solution.py:757
  16.1 0.0 copy-done.1
  16.1 0.0 copy-done
  16.1 5.0 %write.1 = bf16[512,5120]{1,0:T(8,128)(2,1)} custom-call(bf16[512,256]{1,0:T(8,128)(2,1)S(1)} %get-tuple-element.10.lhs, bf16[256,5120]{1,0:T(8,128)(2,1)S(1)} %get-tuple-element.11.both, f32[1,5120]{1,0:T(1,128)S(1)} %get-tuple-element.12.bias, f32[512,128]{1,0:T(8,128)S(1)} %get-tuple-element.13.mean, f32[512,128]{1,0:T(8,128)S(1)} %get-tuple-element.14.inv, ...), custom_call_target="tpu_custom_call" | custom-call | tf_op jit(solution)/shard_map/write/pallas_call | solution.py:805
Async XLA Ops:
  0.0 16.1 %copy-start.1 = (f32[5120]{0:T(1024)S(1)}, f32[5120]{0:T(1024)}, u32[]{:S(2)}) copy-start(f32[5120]{0:T(1024)} %param.27) | copy-start | bytes 61444
  0.0 16.1 %copy-start = (f32[5120]{0:T(1024)S(1)}, f32[5120]{0:T(1024)}, u32[]{:S(2)}) copy-start(f32[5120]{0:T(1024)} %param.26) | copy-start | bytes 61444

commit v2 on v0

--- a/solution.py
+++ b/solution.py
@@ -428,9 +428,539 @@
     )(noisy_tokens.T, mask_tokens, lat, patch_weight, context_weight, *vecs)
 
 
+def fold_taps(cw_ref, mw_ref, wt):
+    z, zo = mw_ref.shape
+    channels = cw_ref.shape[1]
+    mw = mw_ref[...]
+    high = mw.astype(BF16)
+    low = (mw - high.astype(F32)).astype(BF16)
+    spread = ones_where((4 * z, z), lambda i, j: i % z == j).astype(BF16)
+    copier = ones_where((zo, K * zo), lambda i, j: j % zo == i).astype(BF16)
+
+    def right_slot(i, j):
+        slot, e = i // z, j // zo
+        return ((slot == 0) & (e == 1)) | ((slot == 2) & (e == 0)) | ((slot == 3) & (e == 2))
+
+    keep = ones_where((4 * z, K * zo), right_slot)
+    parts = []
+    for part in (high, low):
+        tall = jnp.dot(spread, part, preferred_element_type=F32).astype(BF16)
+        parts.append((jnp.dot(tall, copier, preferred_element_type=F32) * keep).astype(BF16))
+    nothing = jnp.zeros((z, channels), BF16)
+    for a in range(K):
+        for b in range(K):
+            at = (a * K + b) * K * zo
+            tap = cw_ref[at : at + K * zo, :]
+            res = jnp.dot(parts[0], tap, preferred_element_type=F32)
+            res = res + jnp.dot(parts[1], tap, preferred_element_type=F32)
+            res = res.astype(BF16)
+            for f in range(2):
+                for slot in range(4):
+                    row = slot * 4 * z + (f + 2 - a) * z
+                    wt[row : row + z, (f * K + b) * channels : (f * K + b + 1) * channels] = res[
+                        slot * z : (slot + 1) * z
+                    ]
+    for b in range(K):
+        for slot in range(4):
+            row = slot * 4 * z
+            wt[row + 3 * z : row + 4 * z, b * channels : (b + 1) * channels] = nothing
+            wt[row : row + z, (K + b) * channels : (K + b + 1) * channels] = nothing
+
+
+def halves(v):
+    high = v.astype(BF16)
+    return high, (v - high.astype(F32)).astype(BF16)
+
+
+def send_kernel(
+    sizes, x_hbm, cw_hbm, gain_hbm, mw_hbm, cb_hbm, mb_hbm, noisy_hbm, mask_hbm, pw_hbm, xw_hbm, pb_hbm,
+    xb_hbm, scale_hbm, lhs_ref, late_ref, early_ref, inv_ref,
+    cwt, gain_ref, mw_ref, cb_ref, mb_ref, pb_ref, xb_ref, scale_ref, wt, xin, actf, cen, edge, stack, msg, got,
+    lat_w, both, own, gram, own_gram, order, swap, bias_row, center, late_mean, x_early, base, in_sem, s_sem, r_sem,
+):
+    n_c, n_s, n_t, shard_rows = sizes
+    c, s, t = lax.axis_index("cfg"), lax.axis_index("seq"), lax.axis_index("tile")
+    frames, height, columns, channels = x_hbm.shape
+    half = height // n_c
+    pairs = half // 2
+    z = mw_ref.shape[0]
+    chunks = pairs // shard_rows
+    reach = frames + K - 1
+    split = 4 * z
+    width = late_ref.shape[1]
+    tokens = lhs_ref.shape[0]
+    depth = pw_hbm.shape[0] + xw_hbm.shape[0]
+
+    def dev(ci, si, ti):
+        return {"cfg": ci, "seq": si, "tile": ti}
+
+    cut = half // 2 + 2
+    start = c * (half - 1)
+    xs = [
+        pltpu.make_async_copy(
+            x_hbm.at[:, pl.ds(start + lo, size)], xin.at[:, pl.ds(1 - c + lo, size)], in_sem.at[i]
+        )
+        for i, (lo, size) in enumerate(((0, cut), (cut, half + 1 - cut)))
+    ]
+    small = [
+        pltpu.make_async_copy(src, dst, in_sem.at[2 + i])
+        for i, (src, dst) in enumerate(
+            ((gain_hbm, gain_ref), (mw_hbm, mw_ref), (cb_hbm, cb_ref), (mb_hbm, mb_ref), (cw_hbm, cwt))
+        )
+    ]
+    later = [
+        pltpu.make_async_copy(src, dst, in_sem.at[7 + i])
+        for i, (src, dst) in enumerate(
+            (
+                (pb_hbm, pb_ref), (xb_hbm, xb_ref), (scale_hbm, scale_ref), (noisy_hbm, own),
+                (mask_hbm, x_early.at[:, 2 * split :]), (xw_hbm.at[:split], lat_w),
+                (pw_hbm, both.at[:split]), (xw_hbm.at[split:], both.at[2 * split : depth]),
+            )
+        )
+    ]
+    xs[0].start()
+    for load in small:
+        load.start()
+    xs[1].start()
+
+    barrier = pltpu.get_barrier_semaphore()
+    first = (s * n_t + t) * shard_rows
+    frame = first // (height // 2)
+    src_t = frame // frames
+    src_c = first % (height // 2) // pairs
+    carried = (src_t > 0) & (frame % frames < K - 1)
+    for si in range(n_s):
+        for back in range(2):
+            mine = (src_c == c) & (src_t - back == t) & (s == si)
+            wanted = jnp.logical_not(mine)
+            if back:
+                wanted = wanted & carried
+
+            @pl.when(wanted)
+            def _():
+                pl.semaphore_signal(
+                    barrier, inc=1, device_id=dev(src_c, si, src_t - back), device_id_type=MESH
+                )
+
+    def place(g, m):
+        shard = ((t * frames + g) * (height // 2) + c * pairs) // shard_rows + m
+        return shard // n_t, shard % n_t
+
+    own_main = (src_c == c) & (src_t == t)
+    own_carry = (src_c == c) & (src_t - 1 == t) & carried
+    more = t + 1 < n_t
+    expect = frames * chunks * n_c - own_main.astype(jnp.int32)
+    rest = (reach - frames) * chunks * n_c - own_carry.astype(jnp.int32)
+    expect = expect + jnp.where(more, rest, 0)
+
+    zero_row = jnp.zeros((frames, 1, columns, channels), BF16)
+
+    @pl.when(c == 0)
+    def _():
+        xin[:, 0:1] = zero_row
+
+    @pl.when(c == n_c - 1)
+    def _():
+        xin[:, half + 1 : half + 2] = zero_row
+
+    def activate(lo, hi):
+        step = 2
+        for f in range(frames):
+            for r in range(lo, hi, step):
+                v = xin[f, r : r + step].astype(F32).reshape(step * columns, channels)
+                energy = jnp.sum(v * v, axis=-1, keepdims=True) * (1.0 / channels)
+                v = v * lax.rsqrt(energy + 1e-06) * gain
+                actf[f, r * columns : (r + step) * columns, :] = v + v * jnp.tanh(v)
+
+    count = half * columns // 2
+
+    def convolve(m):
+        lo = m * count
+        for f in range(frames):
+            taps = [actf[f, lo + b * columns : lo + b * columns + count, :].astype(BF16) for b in range(K)]
+            total = nt(jnp.concatenate(taps, axis=1), wt[:, f * K * channels : (f + 1) * K * channels])
+            cen[f, lo : lo + count, :] = total[:, :128]
+            edge[f, lo : lo + count, :] = total[:, 128:]
+
+    def both_frames(ref, at):
+        v = ref[0, pl.ds(at, 8, stride=2 * columns), :]
+        for f in range(1, frames):
+            v = v + ref[f, pl.ds(at, 8, stride=2 * columns), :]
+        return v
+
+    lane = lax.broadcasted_iota(jnp.int32, (8, 128), 1)
+    upper = lane >= 64
+    one = lane // z % 2 == 1
+    two = lane // z % 4 >= 2
+
+    def pack(m):
+        cols = {}
+        for a in range(2):
+            mids, rights, lefts = [], [], []
+            for w in range(columns):
+                starts = [((m * shard_rows + h * 8) * 2 + a) * columns + w for h in range(2)]
+                c0, c1 = (both_frames(cen, at) for at in starts)
+                e0, e1 = (both_frames(edge, at) for at in starts)
+                mids.append(jnp.where(upper, pltpu.roll(c1, 64, 1), c0))
+                turned = pltpu.roll(jnp.where(upper, e0, e1), 64, 1)
+                rights.append(jnp.where(upper, turned, e0))
+                lefts.append(jnp.where(upper, e1, turned))
+            for w in range(columns):
+                v = mids[w]
+                if w > 0:
+                    v = v + rights[w - 1]
+                if w < columns - 1:
+                    v = v + lefts[w + 1]
+                cols[a, w] = v
+            cols[a, columns] = rights[columns - 1]
+            cols[a, columns + 1] = lefts[0]
+        for j in range(columns // 2 + 1):
+            p = [cols[a, 2 * j + b] for b in range(2) for a in range(2)]
+            q = [None] * 4
+            for k in (0, 2):
+                q[k] = jnp.where(one, pltpu.roll(p[k + 1], z, 1), p[k])
+                q[k + 1] = jnp.where(one, p[k + 1], pltpu.roll(p[k], 128 - z, 1))
+            for k in range(2):
+                low = jnp.where(two, pltpu.roll(q[k + 2], 2 * z, 1), q[k])
+                high = jnp.where(two, q[k + 2], pltpu.roll(q[k], 128 - 2 * z, 1))
+                msg[k * chunks + m, j * 8 : j * 8 + 8, :] = low.astype(BF16)
+                msg[(k + 2) * chunks + m, j * 8 : j * 8 + 8, :] = high.astype(BF16)
+
+    def send(m):
+        def post(g):
+            si, ti = place(g, m)
+            here = (si == s) & (ti == t)
+            slot = g // frames
+            src, dst = msg.at[g * chunks + m], got.at[slot, s]
+            for ci in range(n_c):
+
+                @pl.when(here & (c == ci))
+                def _():
+                    pltpu.make_async_copy(src, dst, r_sem.at[slot]).start()
+
+                @pl.when(jnp.logical_not(here & (c == ci)))
+                def _():
+                    pltpu.make_async_remote_copy(
+                        src_ref=src, dst_ref=dst, send_sem=s_sem.at[slot, ci], recv_sem=r_sem.at[slot],
+                        device_id=dev(ci, si, ti), device_id_type=MESH,
+                    ).start()
+
+        for g in range(frames):
+            post(g)
+
+        @pl.when(more)
+        def _():
+            for g in range(frames, reach):
+                post(g)
+
+    per = columns // 2 * 8
+    n = n_s * per
+    cols = columns // 2
+    with jax.named_scope("tables"):
+        i = lax.broadcasted_iota(jnp.int32, (n, n), 0)
+        j = lax.broadcasted_iota(jnp.int32, (n, n), 1)
+        wanted = ((i & (cols * n_s - 1)) // cols) * per + (i & (cols - 1)) * 8 + i // (cols * n_s)
+        order[...] = jnp.where(j == wanted, 1.0, 0.0).astype(BF16)
+        i = lax.broadcasted_iota(jnp.int32, (split, split), 0)
+        j = lax.broadcasted_iota(jnp.int32, (split, split), 1)
+        swap[...] = jnp.where(j == (i & (z - 1)) * 4 + (i // z & 1) * 2 + i // (2 * z), 1.0, 0.0).astype(BF16)
+    with jax.named_scope("load0"):
+        for load in small[:4]:
+            load.wait()
+    with jax.named_scope("loadx"):
+        xs[0].wait()
+    with jax.named_scope("loadt"):
+        small[4].wait()
+        for load in later:
+            load.start()
+    with jax.named_scope("fold"):
+        gain = gain_ref[...].reshape(1, channels) * 0.5
+        fold_taps(cwt, mw_ref, wt)
+        activate(0, half // 2 + 2)
+    with jax.named_scope("load1"):
+        xs[1].wait()
+    with jax.named_scope("conv0"):
+        convolve(0)
+        activate(half // 2 + 2, half + 2)
+        pack(0)
+    ahead = ((s == 0) & (t == 0)).astype(jnp.int32)
+    block = 128
+
+    @pl.loop(0, 2)
+    def _(turn):
+        @pl.when(turn == ahead)
+        def _():
+            with jax.named_scope("barrierwait"):
+                pl.semaphore_wait(barrier, expect)
+            with jax.named_scope("send0"):
+                send(0)
+
+        @pl.when(turn == 0)
+        def _():
+            with jax.named_scope("conv1"):
+                convolve(1)
+                pack(1)
+
+        @pl.when(turn == ahead)
+        def _():
+            with jax.named_scope("send1"):
+                send(1)
+
+        @pl.when(turn == 1 - ahead)
+        def _():
+            with jax.named_scope("loadw"):
+                for load in later:
+                    load.wait()
+            with jax.named_scope("prep"):
+                bias_row[...] = fold_bias(mw_ref, cb_ref, mb_ref)
+                b = pb_ref[...] + xb_ref[...]
+                b = b - jnp.sum(b, axis=-1, keepdims=True) * (1.0 / width)
+                scaled = scale_ref[...] + 1.0
+                center[0] = b
+                center[1] = scaled
+                step = 512
+                row = lax.broadcasted_iota(jnp.int32, (16, step), 0)
+                for k in range(0, width, step):
+                    at = slice(k, k + step)
+                    part = jnp.dot(swap[...], lat_w[:, at], preferred_element_type=F32)
+                    both[split : 2 * split, at] = part.astype(BF16)
+                    high, low = halves(part * scaled[:, at])
+                    late_ref[:split, at] = high
+                    late_ref[split : 2 * split, at] = low
+                    high = scaled[:, at].astype(BF16).astype(F32)
+                    low = scaled[:, at] - high
+                    four = jnp.where(row % 2 == 0, high, low)
+                    late_ref[2 * split :, at] = jnp.where(row < 4, four, 0.0).astype(BF16)
+                high = b.astype(BF16).astype(F32)
+                mid = (b - high).astype(BF16).astype(F32)
+                row = lax.broadcasted_iota(jnp.int32, (16, width), 0)
+                picked = jnp.where(row == 0, 1.0, jnp.where(row == 1, high, jnp.where(row == 2, mid, b - high - mid)))
+                both[depth:, :] = jnp.where(row < 4, picked, 0.0).astype(BF16)
+                noise = own[...].astype(F32).T
+                x_early[:, : 2 * split] = jnp.concatenate([noise, jnp.zeros_like(noise)], axis=1).astype(BF16)
+            with jax.named_scope("gram"):
+                for part in range(2):
+                    at = slice(part * (width // 2), (part + 1) * (width // 2))
+                    probe = jnp.concatenate([both[split : 2 * split, at], both[depth:, at]], axis=0)
+                    gram[part] = nt(probe, both[:depth, at])
+                square = gram[0] + gram[1]
+                sums = square[split:]
+                wmean = sums[0:1] * (1.0 / width)
+                cross = (sums[1:2] + sums[2:3] + sums[3:4]) * 2.0
+                high, low = halves(square[:split])
+                own_gram[:split, :] = high[:, : 2 * split]
+                own_gram[split:, :] = low[:, : 2 * split]
+                late_mean[...] = wmean[:, : 2 * split]
+                pair_high = jnp.concatenate([high, high], axis=0)
+                pair_low = jnp.concatenate([low, low], axis=0)
+                for k in range(0, tokens, block):
+                    at = slice(k, k + block)
+                    x = x_early[at, :]
+                    y = nt(x, pair_high) + nt(x, pair_low)
+                    mean = jnp.sum(x.astype(F32) * wmean, axis=-1, keepdims=True)
+                    base[0, at, :] = jnp.broadcast_to(mean, (block, 128))
+                    base[2, at, :] = 2.0 * y + cross[:, : 2 * split]
+
+    with jax.named_scope("early"):
+        step = 256
+        for k in range(0, width, step):
+            at = slice(k, k + step)
+            part = jnp.dot(x_early[...], both[:depth, at], preferred_element_type=F32) + center[0, :, at]
+            early_ref[:, at] = part * center[1, :, at]
+            square = part * part
+            square = square[:, :128] + square[:, 128:]
+            if k == 0:
+                base[1] = square
+            else:
+                base[1] = base[1] + square
+
+    def drain(slot, own_piece):
+        total = (frames if slot == 0 else reach - frames) * chunks
+        for ci in range(n_c):
+            less = own_piece & (c == ci)
+
+            @pl.when(less)
+            def _():
+                part = msg.at[: total - 1]
+                pltpu.make_async_copy(part, part, s_sem.at[slot, ci]).wait()
+
+            @pl.when(jnp.logical_not(less))
+            def _():
+                part = msg.at[:total]
+                pltpu.make_async_copy(part, part, s_sem.at[slot, ci]).wait()
+
+    with jax.named_scope("drain"):
+        drain(0, own_main)
+
+        @pl.when(more)
+        def _():
+            drain(1, own_carry)
+
+    with jax.named_scope("recv"):
+
+        @pl.when(carried)
+        def _():
+            pltpu.make_async_copy(got.at[1], got.at[1], r_sem.at[1]).wait()
+
+        pltpu.make_async_copy(got.at[0], got.at[0], r_sem.at[0]).wait()
+
+    with jax.named_scope("assemble"):
+        odd = lane // (2 * z) % 2 == 1
+
+        def strip(slot, si):
+            v = got[slot, si, :per, :].astype(F32)
+            parts = [v[k : k + 8] for k in range(0, per, 8)]
+            if si > 0:
+                parts[0] = parts[0] + jnp.where(odd, 0.0, got[slot, si - 1, per:, :].astype(F32))
+            if si < n_s - 1:
+                parts[-1] = parts[-1] + jnp.where(odd, got[slot, si + 1, per:, :].astype(F32), 0.0)
+            return jnp.concatenate(parts, axis=0)
+
+        for si in range(n_s):
+            stack[si * per : (si + 1) * per, :] = strip(0, si) + bias_row[...]
+
+        @pl.when(carried)
+        def _():
+            for si in range(n_s):
+                at = slice(si * per, (si + 1) * per)
+                stack[at, :] = stack[at, :] + strip(1, si)
+
+        placed = jnp.dot(order[...], stack[...].astype(BF16), preferred_element_type=F32)
+        turned = pltpu.roll(placed, 64, 1)
+        low = lax.broadcasted_iota(jnp.int32, (n, 128), 1) < 64
+        twice = [jnp.where(low, placed, turned), jnp.where(low, turned, placed)]
+        for h in range(2):
+            lhs_ref[h * n : (h + 1) * n, : 2 * split] = twice[h].astype(BF16)
+
+    with jax.named_scope("stats"):
+        for k in range(0, tokens, block):
+            at = slice(k, k + block)
+            x = lhs_ref[at, : 2 * split]
+            y = jnp.dot(x, own_gram[...], preferred_element_type=F32) + base[2, at, :]
+            wide_lane = lax.broadcasted_iota(jnp.int32, (block, 128), 1)
+            x = jnp.where(wide_lane < split, 0.0, x.astype(F32))
+            mean = jnp.sum(x * late_mean[...], axis=-1, keepdims=True) + base[0, at, :]
+            power = jnp.sum(x * y + base[1, at, :], axis=-1, keepdims=True)
+            variance = jnp.maximum(power * (1.0 / width) - mean * mean, 0.0)
+            inv_ref[at, :] = lax.rsqrt(variance + 1e-06)
+            high = mean.astype(BF16).astype(F32)
+            pair = jnp.where(wide_lane < 2, high, mean - high)
+            lhs_ref[at, 2 * split :] = jnp.where(wide_lane < 4, -pair, 0.0).astype(BF16)
+
+
+def write_kernel(lhs, late, early, inv, shift, out, buf, sem):
+    width = buf.shape[1]
+    wide = 512 if width % 512 == 0 else width
+    step = min(wide, 256)
+    copies = []
+    for k in range(0, width, wide):
+        for q in range(k, k + wide, step):
+            at = slice(q, q + step)
+            part = jnp.dot(lhs[:, : late.shape[0]], late[:, at], preferred_element_type=F32)
+            factor = jnp.concatenate([inv[...]] * (step // 128), axis=1)
+            buf[:, at] = ((part + early[:, at]) * factor + shift[:, at]).astype(BF16)
+        copy = pltpu.make_async_copy(buf.at[:, k : k + wide], out.at[:, k : k + wide], sem.at[k // wide])
+        copy.start()
+        copies.append(copy)
+    for copy in copies:
+        copy.wait()
+
+
+def fast(
+    section_input, norm_gain, conv_weight, conv_bias, mean_weight, mean_bias, noisy_tokens,
+    mask_tokens, patch_weight, patch_bias, context_weight, context_bias, norm_shift, norm_scale,
+):
+    frames, height, columns, channels = section_input.shape
+    n_c, n_s, n_t = lax.axis_size("cfg"), lax.axis_size("seq"), lax.axis_size("tile")
+    z = mean_weight.shape[1]
+    tokens, width = noisy_tokens.shape[0], patch_weight.shape[1]
+    shard_rows = tokens // (n_s * columns // 2)
+    half = height // n_c
+    count = half * columns
+    chunks = half // 2 // shard_rows
+    reach = frames + K - 1
+    per = (columns // 2 + 1) * 8
+    depth = patch_weight.shape[0] + context_weight.shape[0]
+    split = 4 * z
+    n = n_s * columns // 2 * 8
+    vmem = pl.BlockSpec(memory_space=pltpu.VMEM)
+    hbm = pl.BlockSpec(memory_space=pltpu.HBM)
+    args = (
+        section_input, conv_weight.T, norm_gain, mean_weight.T, conv_bias[None], mean_bias[None],
+        noisy_tokens.T, mask_tokens, patch_weight, context_weight, patch_bias[None], context_bias[None],
+        norm_scale[None],
+    )
+    prepared = pl.pallas_call(
+        functools.partial(send_kernel, (n_c, n_s, n_t, shard_rows)),
+        out_shape=(
+            pltpu.VMEM((tokens, 2 * split + 128), BF16),
+            pltpu.VMEM((2 * split + 16, width), BF16),
+            pltpu.VMEM((tokens, width), F32),
+            pltpu.VMEM((tokens, 128), F32),
+        ),
+        in_specs=[hbm] * len(args),
+        out_specs=(vmem,) * 4,
+        scratch_shapes=[
+            pltpu.VMEM(conv_weight.shape[::-1], BF16),
+            pltpu.VMEM((channels,), F32),
+            pltpu.VMEM(mean_weight.shape[::-1], F32),
+            pltpu.VMEM((1, conv_bias.shape[0]), F32),
+            pltpu.VMEM((1, z), F32),
+            pltpu.VMEM((1, width), F32),
+            pltpu.VMEM((1, width), F32),
+            pltpu.VMEM((1, width), F32),
+            pltpu.VMEM((16 * z, frames * K * channels), BF16),
+            pltpu.VMEM((frames, half + 2, columns, channels), BF16),
+            pltpu.VMEM((frames, (half + 2) * columns, channels), F32),
+            pltpu.VMEM((frames, count, 128), F32),
+            pltpu.VMEM((frames, count, 128), F32),
+            pltpu.VMEM((n, 128), F32),
+            pltpu.VMEM((reach * chunks, per, 128), BF16),
+            pltpu.VMEM((2, n_s, per, 128), BF16),
+            pltpu.VMEM((split, width), BF16),
+            pltpu.VMEM((depth + 16, width), BF16),
+            pltpu.VMEM(noisy_tokens.shape[::-1], BF16),
+            pltpu.VMEM((2, split + 16, depth), F32),
+            pltpu.VMEM((2 * split, 2 * split), BF16),
+            pltpu.VMEM((n, n), BF16),
+            pltpu.VMEM((split, split), BF16),
+            pltpu.VMEM((1, 128), F32),
+            pltpu.VMEM((2, 1, width), F32),
+            pltpu.VMEM((1, 128), F32),
+            pltpu.VMEM((tokens, depth), BF16),
+            pltpu.VMEM((3, tokens, 128), F32),
+            pltpu.SemaphoreType.DMA((15,)),
+            pltpu.SemaphoreType.DMA((2, n_c)),
+            pltpu.SemaphoreType.DMA((2,)),
+        ],
+        compiler_params=pltpu.CompilerParams(
+            collective_id=0, has_side_effects=True, vmem_limit_bytes=32 * 2**20
+        ),
+        name="send",
+    )(*(pltpu.with_memory_space_constraint(v, pltpu.HBM) for v in args))
+    return pl.pallas_call(
+        write_kernel,
+        out_shape=jax.ShapeDtypeStruct((tokens, width), BF16),
+        in_specs=[vmem] * 5,
+        out_specs=hbm,
+        scratch_shapes=[pltpu.VMEM((tokens, width), BF16), pltpu.SemaphoreType.DMA((max(1, width // 512),))],
+        compiler_params=pltpu.CompilerParams(vmem_limit_bytes=24 * 2**20),
+        name="write",
+    )(*prepared, norm_shift[None])
+
+
+def choose(*args):
+    n_c, n_s, n_t = lax.axis_size("cfg"), lax.axis_size("seq"), lax.axis_size("tile")
+    frames, height, columns, _ = args[0].shape
+    rows = args[6].shape[0] // (n_s * columns // 2)
+    fits = columns == 8 and args[4].shape[1] == 16 and frames == 2 and rows == 16
+    fits = fits and height // n_c == 4 * rows
+    return fast(*args) if fits else body(*args)
+
+
 def solution(mesh):
     placed = (P("tile", None, "seq", None),) + (P(),) * 5
     placed = placed + (P(("seq", "tile"), None),) * 2 + (P(),) * 6
     return jax.shard_map(
-        body, mesh=mesh, in_specs=placed, out_specs=P(("seq", "tile"), None), check_vma=False
+        choose, mesh=mesh, in_specs=placed, out_specs=P(("seq", "tile"), None), check_vma=False
     )

time: 29.8 us -> 14.4 us (0.48)
  the two profiles are of different devices: /device:TPU:0 before, /device:TPU:5 now
where the time goes in v2:
time: 14.4 us; the launch traced here: 14.3 us
  Pallas kernels  14.2 us (99%)
    pallas_call x1, Pallas kernels, fast(): pl.pallas_call(functools.partial(send_kernel, (n_c, n_s, n_t, shard_rows)...  11.5 us
    pallas_call x1, Pallas kernels, fast(): pl.pallas_call(write_kernel, out_shape=jax.ShapeDtypeStruct((tokens, widt...  2.71 us

profile of v2, /device:TPU:5, one launch (start us, length us, event | category | flops | bytes accessed | tf_op | source)
XLA Modules:
  0.0 14.3 jit_solution(10755019101237545981)
XLA Ops:
  0.0 0.0 copy-start
  0.0 11.5 %send.1 = (bf16[512,256]{1,0:T(8,128)(2,1)S(1)}, bf16[144,5120]{1,0:T(8,128)(2,1)S(1)}, f32[512,5120]{1,0:T(8,128)S(1)}, f32[512,128]{1,0:T(8,128)S(1)}) custom-call(bf16[2,128,8,384]{3,2,1,0:T(8,128)(2,1)} %x_hbm.1, bf16[864,384]{1,0:T(8,128)(2,1)} %bitcast.10, f32[384]{0:T(512)} %gain_hbm.1, f32[16,32]{1,0:T(8,128)} %bitcast.15, f32[1,32]{1,0:T(1,128)} %bitcast.16, ...), custom_call_target="tpu_custom_call" | custom-call | tf_op jit(solution)/shard_map/send/pallas_call | solution.py:893
  11.5 0.0 copy-done
  11.5 2.7 %write.1 = bf16[512,5120]{1,0:T(8,128)(2,1)} custom-call(bf16[512,256]{1,0:T(8,128)(2,1)S(1)} %get-tuple-element.9.lhs, bf16[144,5120]{1,0:T(8,128)(2,1)S(1)} %get-tuple-element.10.late, f32[512,5120]{1,0:T(8,128)S(1)} %get-tuple-element.11.early, f32[512,128]{1,0:T(8,128)S(1)} %get-tuple-element.12.inv, f32[1,5120]{1,0:T(1,128)S(1)} %bitcast.9), custom_call_target="tpu_custom_call" | custom-call | tf_op jit(solution)/shard_map/write/pallas_call | solution.py:941
Async XLA Ops:
  0.0 11.5 %copy-start = (f32[5120]{0:T(1024)S(1)}, f32[5120]{0:T(1024)}, u32[]{:S(2)}) copy-start(f32[5120]{0:T(1024)} %param.26) | copy-start | bytes 61444

commit v3 on v2

--- a/solution.py
+++ b/solution.py
@@ -428,43 +428,41 @@
     )(noisy_tokens.T, mask_tokens, lat, patch_weight, context_weight, *vecs)
 
 
-def fold_taps(cw_ref, mw_ref, wt):
+def fold_parts(mw_ref):
     z, zo = mw_ref.shape
+    wide = jnp.concatenate([mw_ref[...]] * K, axis=1)
+    tap = lax.broadcasted_iota(jnp.int32, wide.shape, 1) // zo
+    tall = jnp.concatenate([jnp.where(tap == e, wide, 0.0) for e in (1, 0, 2)], axis=0)
+    high = tall.astype(BF16).astype(F32)
+    return jnp.concatenate([high, tall - high], axis=1).astype(BF16)
+
+
+def fold_taps(cw_ref, parts, wt, z, outer):
     channels = cw_ref.shape[1]
-    mw = mw_ref[...]
-    high = mw.astype(BF16)
-    low = (mw - high.astype(F32)).astype(BF16)
-    spread = ones_where((4 * z, z), lambda i, j: i % z == j).astype(BF16)
-    copier = ones_where((zo, K * zo), lambda i, j: j % zo == i).astype(BF16)
-
-    def right_slot(i, j):
-        slot, e = i // z, j // zo
-        return ((slot == 0) & (e == 1)) | ((slot == 2) & (e == 0)) | ((slot == 3) & (e == 2))
-
-    keep = ones_where((4 * z, K * zo), right_slot)
-    parts = []
-    for part in (high, low):
-        tall = jnp.dot(spread, part, preferred_element_type=F32).astype(BF16)
-        parts.append((jnp.dot(tall, copier, preferred_element_type=F32) * keep).astype(BF16))
-    nothing = jnp.zeros((z, channels), BF16)
-    for a in range(K):
+    size = parts.shape[1] // 2
+    for a in outer:
         for b in range(K):
-            at = (a * K + b) * K * zo
-            tap = cw_ref[at : at + K * zo, :]
-            res = jnp.dot(parts[0], tap, preferred_element_type=F32)
-            res = res + jnp.dot(parts[1], tap, preferred_element_type=F32)
+            at = (a * K + b) * size
+            tap = cw_ref[at : at + size, :]
+            res = jnp.dot(parts, jnp.concatenate([tap, tap], axis=0), preferred_element_type=F32)
             res = res.astype(BF16)
             for f in range(2):
-                for slot in range(4):
+                for k, slot in enumerate((0, 2, 3)):
                     row = slot * 4 * z + (f + 2 - a) * z
                     wt[row : row + z, (f * K + b) * channels : (f * K + b + 1) * channels] = res[
-                        slot * z : (slot + 1) * z
+                        k * z : (k + 1) * z
                     ]
-    for b in range(K):
-        for slot in range(4):
-            row = slot * 4 * z
-            wt[row + 3 * z : row + 4 * z, b * channels : (b + 1) * channels] = nothing
-            wt[row : row + z, (K + b) * channels : (K + b + 1) * channels] = nothing
+
+
+def fold_zeros(wt, z, channels):
+    deep = K * channels
+    for slot in range(4):
+        row = slot * 4 * z
+        if slot == 1:
+            wt[row : row + 4 * z, :] = jnp.zeros((4 * z, 2 * deep), BF16)
+        else:
+            wt[row + 3 * z : row + 4 * z, :deep] = jnp.zeros((z, deep), BF16)
+            wt[row : row + z, deep:] = jnp.zeros((z, deep), BF16)
 
 
 def halves(v):
@@ -475,7 +473,7 @@
 def send_kernel(
     sizes, x_hbm, cw_hbm, gain_hbm, mw_hbm, cb_hbm, mb_hbm, noisy_hbm, mask_hbm, pw_hbm, xw_hbm, pb_hbm,
     xb_hbm, scale_hbm, lhs_ref, late_ref, early_ref, inv_ref,
-    cwt, gain_ref, mw_ref, cb_ref, mb_ref, pb_ref, xb_ref, scale_ref, wt, xin, actf, cen, edge, stack, msg, got,
+    cwt, gain_ref, mw_ref, cb_ref, mb_ref, pb_ref, xb_ref, scale_ref, wt, xin, actf, cen, edge, msg, got,
     lat_w, both, own, gram, own_gram, order, swap, bias_row, center, late_mean, x_early, base, in_sem, s_sem, r_sem,
 ):
     n_c, n_s, n_t, shard_rows = sizes
@@ -497,19 +495,31 @@
     cut = half // 2 + 2
     start = c * (half - 1)
     xs = [
-        pltpu.make_async_copy(
-            x_hbm.at[:, pl.ds(start + lo, size)], xin.at[:, pl.ds(1 - c + lo, size)], in_sem.at[i]
-        )
+        [
+            pltpu.make_async_copy(
+                x_hbm.at[f, pl.ds(start + lo, size)],
+                xin.at[f, pl.ds(1 - c + lo, size)],
+                in_sem.at[i * frames + f],
+            )
+            for f in range(frames)
+        ]
         for i, (lo, size) in enumerate(((0, cut), (cut, half + 1 - cut)))
     ]
+    third = cw_hbm.shape[0] // K
+    taps = [
+        pltpu.make_async_copy(
+            cw_hbm.at[a * third : (a + 1) * third], cwt.at[a * third : (a + 1) * third], in_sem.at[4 + a]
+        )
+        for a in range(K)
+    ]
     small = [
-        pltpu.make_async_copy(src, dst, in_sem.at[2 + i])
+        pltpu.make_async_copy(src, dst, in_sem.at[7 + i])
         for i, (src, dst) in enumerate(
-            ((gain_hbm, gain_ref), (mw_hbm, mw_ref), (cb_hbm, cb_ref), (mb_hbm, mb_ref), (cw_hbm, cwt))
+            ((gain_hbm, gain_ref), (mw_hbm, mw_ref), (cb_hbm, cb_ref), (mb_hbm, mb_ref))
         )
     ]
     later = [
-        pltpu.make_async_copy(src, dst, in_sem.at[7 + i])
+        pltpu.make_async_copy(src, dst, in_sem.at[11 + i])
         for i, (src, dst) in enumerate(
             (
                 (pb_hbm, pb_ref), (xb_hbm, xb_ref), (scale_hbm, scale_ref), (noisy_hbm, own),
@@ -518,10 +528,16 @@
             )
         )
     ]
-    xs[0].start()
-    for load in small:
+    small[1].start()
+    for load in taps:
         load.start()
-    xs[1].start()
+    for load in xs[0]:
+        load.start()
+    small[0].start()
+    for load in xs[1]:
+        load.start()
+    small[2].start()
+    small[3].start()
 
     barrier = pltpu.get_barrier_semaphore()
     first = (s * n_t + t) * shard_rows
@@ -568,8 +584,8 @@
         for f in range(frames):
             for r in range(lo, hi, step):
                 v = xin[f, r : r + step].astype(F32).reshape(step * columns, channels)
-                energy = jnp.sum(v * v, axis=-1, keepdims=True) * (1.0 / channels)
-                v = v * lax.rsqrt(energy + 1e-06) * gain
+                energy = jnp.sum(v * v, axis=-1, keepdims=True)
+                v = v * lax.rsqrt(energy + 1e-06 * channels) * gain
                 actf[f, r * columns : (r + step) * columns, :] = v + v * jnp.tanh(v)
 
     count = half * columns // 2
@@ -664,31 +680,38 @@
         i = lax.broadcasted_iota(jnp.int32, (split, split), 0)
         j = lax.broadcasted_iota(jnp.int32, (split, split), 1)
         swap[...] = jnp.where(j == (i & (z - 1)) * 4 + (i // z & 1) * 2 + i // (2 * z), 1.0, 0.0).astype(BF16)
-    with jax.named_scope("load0"):
-        for load in small[:4]:
+        fold_zeros(wt, z, channels)
+    with jax.named_scope("loadt"):
+        small[1].wait()
+        parts = fold_parts(mw_ref)
+        for load in taps:
             load.wait()
+    with jax.named_scope("fold"):
+        fold_taps(cwt, parts, wt, z, range(K))
     with jax.named_scope("loadx"):
-        xs[0].wait()
-    with jax.named_scope("loadt"):
-        small[4].wait()
+        small[0].wait()
+        for load in xs[0]:
+            load.wait()
+    with jax.named_scope("act0"):
+        gain = gain_ref[...].reshape(1, channels) * (0.5 * channels**0.5)
+        activate(0, half // 2 + 2)
         for load in later:
             load.start()
-    with jax.named_scope("fold"):
-        gain = gain_ref[...].reshape(1, channels) * 0.5
-        fold_taps(cwt, mw_ref, wt)
-        activate(0, half // 2 + 2)
-    with jax.named_scope("load1"):
-        xs[1].wait()
     with jax.named_scope("conv0"):
         convolve(0)
-        activate(half // 2 + 2, half + 2)
         pack(0)
-    ahead = ((s == 0) & (t == 0)).astype(jnp.int32)
+    with jax.named_scope("load1"):
+        small[2].wait()
+        small[3].wait()
+        for load in xs[1]:
+            load.wait()
+    ahead = (s < 2).astype(jnp.int32) + ((s == 0) & (t == 0)).astype(jnp.int32)
+    after = (ahead > 0).astype(jnp.int32)
     block = 128
 
     @pl.loop(0, 2)
     def _(turn):
-        @pl.when(turn == ahead)
+        @pl.when(turn == after)
         def _():
             with jax.named_scope("barrierwait"):
                 pl.semaphore_wait(barrier, expect)
@@ -698,15 +721,16 @@
         @pl.when(turn == 0)
         def _():
             with jax.named_scope("conv1"):
+                activate(half // 2 + 2, half + 2)
                 convolve(1)
                 pack(1)
 
-        @pl.when(turn == ahead)
+        @pl.when(turn == after)
         def _():
             with jax.named_scope("send1"):
                 send(1)
 
-        @pl.when(turn == 1 - ahead)
+        @pl.when(turn == (ahead == 0).astype(jnp.int32))
         def _():
             with jax.named_scope("loadw"):
                 for load in later:
@@ -716,41 +740,44 @@
                 b = pb_ref[...] + xb_ref[...]
                 b = b - jnp.sum(b, axis=-1, keepdims=True) * (1.0 / width)
                 scaled = scale_ref[...] + 1.0
-                center[0] = b
-                center[1] = scaled
+                center[...] = scaled
                 step = 512
-                row = lax.broadcasted_iota(jnp.int32, (16, step), 0)
+                whole = None
                 for k in range(0, width, step):
                     at = slice(k, k + step)
                     part = jnp.dot(swap[...], lat_w[:, at], preferred_element_type=F32)
                     both[split : 2 * split, at] = part.astype(BF16)
+                    whole = part if whole is None else whole + part
+                lat_mean = jnp.sum(whole, axis=-1, keepdims=True) * (1.0 / width)
+                late_mean[...] = jnp.broadcast_to(lat_mean, late_mean.shape)
+                for k in range(0, width, step):
+                    at = slice(k, k + step)
+                    part = both[split : 2 * split, at].astype(F32) - lat_mean
                     high, low = halves(part * scaled[:, at])
                     late_ref[:split, at] = high
-                    late_ref[split : 2 * split, at] = low
-                    high = scaled[:, at].astype(BF16).astype(F32)
-                    low = scaled[:, at] - high
-                    four = jnp.where(row % 2 == 0, high, low)
-                    late_ref[2 * split :, at] = jnp.where(row < 4, four, 0.0).astype(BF16)
+                    late_ref[split:, at] = low
                 high = b.astype(BF16).astype(F32)
                 mid = (b - high).astype(BF16).astype(F32)
                 row = lax.broadcasted_iota(jnp.int32, (16, width), 0)
-                picked = jnp.where(row == 0, 1.0, jnp.where(row == 1, high, jnp.where(row == 2, mid, b - high - mid)))
-                both[depth:, :] = jnp.where(row < 4, picked, 0.0).astype(BF16)
+                picked = jnp.where(row == 1, high, jnp.where(row == 2, mid, jnp.where(row == 3, b - high - mid, 1.0)))
+                both[depth : depth + 16, :] = jnp.where(row < 6, picked, 0.0).astype(BF16)
                 noise = own[...].astype(F32).T
                 x_early[:, : 2 * split] = jnp.concatenate([noise, jnp.zeros_like(noise)], axis=1).astype(BF16)
+
+        @pl.when(turn == (ahead < 2).astype(jnp.int32))
+        def _():
             with jax.named_scope("gram"):
                 for part in range(2):
                     at = slice(part * (width // 2), (part + 1) * (width // 2))
-                    probe = jnp.concatenate([both[split : 2 * split, at], both[depth:, at]], axis=0)
+                    probe = jnp.concatenate([both[split : 2 * split, at], both[depth : depth + 16, at]], axis=0)
                     gram[part] = nt(probe, both[:depth, at])
                 square = gram[0] + gram[1]
                 sums = square[split:]
                 wmean = sums[0:1] * (1.0 / width)
                 cross = (sums[1:2] + sums[2:3] + sums[3:4]) * 2.0
-                high, low = halves(square[:split])
+                high, low = halves(square[:split] - late_mean[:, :1] * (wmean * width))
                 own_gram[:split, :] = high[:, : 2 * split]
                 own_gram[split:, :] = low[:, : 2 * split]
-                late_mean[...] = wmean[:, : 2 * split]
                 pair_high = jnp.concatenate([high, high], axis=0)
                 pair_low = jnp.concatenate([low, low], axis=0)
                 for k in range(0, tokens, block):
@@ -758,21 +785,32 @@
                     x = x_early[at, :]
                     y = nt(x, pair_high) + nt(x, pair_low)
                     mean = jnp.sum(x.astype(F32) * wmean, axis=-1, keepdims=True)
-                    base[0, at, :] = jnp.broadcast_to(mean, (block, 128))
-                    base[2, at, :] = 2.0 * y + cross[:, : 2 * split]
+                    high = mean.astype(BF16).astype(F32)
+                    mid = (mean - high).astype(BF16).astype(F32)
+                    spot = lax.broadcasted_iota(jnp.int32, (block, 128), 1) - split
+                    extra = jnp.where(spot == 0, -high, jnp.where(spot == 4, -mid, high + mid - mean))
+                    extra = jnp.where((spot > 0) & (spot < 4), 1.0, extra)
+                    x = x[:, : 2 * split].astype(F32)
+                    x_early[at, : 2 * split] = jnp.where((spot >= 0) & (spot < 6), extra, x).astype(BF16)
+                    base[1, at, :] = 2.0 * y + cross[:, : 2 * split]
 
     with jax.named_scope("early"):
         step = 256
         for k in range(0, width, step):
             at = slice(k, k + step)
-            part = jnp.dot(x_early[...], both[:depth, at], preferred_element_type=F32) + center[0, :, at]
-            early_ref[:, at] = part * center[1, :, at]
+            right = jnp.concatenate(
+                [both[:split, at], both[depth : depth + 16, at], both[: split - 16, at], both[2 * split : depth, at]],
+                axis=0,
+            )
+            part = jnp.dot(x_early[...], right, preferred_element_type=F32)
+            early_ref[:, at] = part * center[:, at]
             square = part * part
             square = square[:, :128] + square[:, 128:]
-            if k == 0:
-                base[1] = square
-            else:
-                base[1] = base[1] + square
+            base[0] = square if k == 0 else base[0] + square
+
+        @pl.when(jnp.logical_not(carried))
+        def _():
+            got[1] = jnp.zeros(got.shape[1:], BF16)
 
     def drain(slot, own_piece):
         total = (frames if slot == 0 else reach - frames) * chunks
@@ -816,36 +854,23 @@
                 parts[-1] = parts[-1] + jnp.where(odd, got[slot, si + 1, per:, :].astype(F32), 0.0)
             return jnp.concatenate(parts, axis=0)
 
-        for si in range(n_s):
-            stack[si * per : (si + 1) * per, :] = strip(0, si) + bias_row[...]
-
-        @pl.when(carried)
-        def _():
-            for si in range(n_s):
-                at = slice(si * per, (si + 1) * per)
-                stack[at, :] = stack[at, :] + strip(1, si)
-
-        placed = jnp.dot(order[...], stack[...].astype(BF16), preferred_element_type=F32)
+        strips = [(strip(0, si) + strip(1, si) + bias_row[...]).astype(BF16) for si in range(n_s)]
+        placed = jnp.dot(order[...], jnp.concatenate(strips, axis=0), preferred_element_type=F32)
         turned = pltpu.roll(placed, 64, 1)
         low = lax.broadcasted_iota(jnp.int32, (n, 128), 1) < 64
         twice = [jnp.where(low, placed, turned), jnp.where(low, turned, placed)]
         for h in range(2):
-            lhs_ref[h * n : (h + 1) * n, : 2 * split] = twice[h].astype(BF16)
+            lhs_ref[h * n : (h + 1) * n, :] = twice[h].astype(BF16)
 
     with jax.named_scope("stats"):
         for k in range(0, tokens, block):
             at = slice(k, k + block)
-            x = lhs_ref[at, : 2 * split]
-            y = jnp.dot(x, own_gram[...], preferred_element_type=F32) + base[2, at, :]
-            wide_lane = lax.broadcasted_iota(jnp.int32, (block, 128), 1)
-            x = jnp.where(wide_lane < split, 0.0, x.astype(F32))
-            mean = jnp.sum(x * late_mean[...], axis=-1, keepdims=True) + base[0, at, :]
-            power = jnp.sum(x * y + base[1, at, :], axis=-1, keepdims=True)
-            variance = jnp.maximum(power * (1.0 / width) - mean * mean, 0.0)
-            inv_ref[at, :] = lax.rsqrt(variance + 1e-06)
-            high = mean.astype(BF16).astype(F32)
-            pair = jnp.where(wide_lane < 2, high, mean - high)
-            lhs_ref[at, 2 * split :] = jnp.where(wide_lane < 4, -pair, 0.0).astype(BF16)
+            x = lhs_ref[at, :]
+            y = jnp.dot(x, own_gram[...], preferred_element_type=F32) + base[1, at, :]
+            upper = lax.broadcasted_iota(jnp.int32, (block, 128), 1) >= split
+            power = jnp.sum(jnp.where(upper, x.astype(F32) * y, 0.0) + base[0, at, :], axis=-1, keepdims=True)
+            variance = jnp.maximum(power * (1.0 / width), 0.0)
+            inv_ref[at, :] = jnp.broadcast_to(lax.rsqrt(variance + 1e-06), (block, 128))
 
 
 def write_kernel(lhs, late, early, inv, shift, out, buf, sem):
@@ -856,7 +881,7 @@
     for k in range(0, width, wide):
         for q in range(k, k + wide, step):
             at = slice(q, q + step)
-            part = jnp.dot(lhs[:, : late.shape[0]], late[:, at], preferred_element_type=F32)
+            part = jnp.dot(lhs[...], late[:, at], preferred_element_type=F32)
             factor = jnp.concatenate([inv[...]] * (step // 128), axis=1)
             buf[:, at] = ((part + early[:, at]) * factor + shift[:, at]).astype(BF16)
         copy = pltpu.make_async_copy(buf.at[:, k : k + wide], out.at[:, k : k + wide], sem.at[k // wide])
@@ -893,8 +918,8 @@
     prepared = pl.pallas_call(
         functools.partial(send_kernel, (n_c, n_s, n_t, shard_rows)),
         out_shape=(
-            pltpu.VMEM((tokens, 2 * split + 128), BF16),
-            pltpu.VMEM((2 * split + 16, width), BF16),
+            pltpu.VMEM((tokens, 2 * split), BF16),
+            pltpu.VMEM((2 * split, width), BF16),
             pltpu.VMEM((tokens, width), F32),
             pltpu.VMEM((tokens, 128), F32),
         ),
@@ -914,7 +939,6 @@
             pltpu.VMEM((frames, (half + 2) * columns, channels), F32),
             pltpu.VMEM((frames, count, 128), F32),
             pltpu.VMEM((frames, count, 128), F32),
-            pltpu.VMEM((n, 128), F32),
             pltpu.VMEM((reach * chunks, per, 128), BF16),
             pltpu.VMEM((2, n_s, per, 128), BF16),
             pltpu.VMEM((split, width), BF16),
@@ -925,11 +949,11 @@
             pltpu.VMEM((n, n), BF16),
             pltpu.VMEM((split, split), BF16),
             pltpu.VMEM((1, 128), F32),
-            pltpu.VMEM((2, 1, width), F32),
-            pltpu.VMEM((1, 128), F32),
+            pltpu.VMEM((1, width), F32),
+            pltpu.VMEM((split, 128), F32),
             pltpu.VMEM((tokens, depth), BF16),
-            pltpu.VMEM((3, tokens, 128), F32),
-            pltpu.SemaphoreType.DMA((15,)),
+            pltpu.VMEM((2, tokens, 128), F32),
+            pltpu.SemaphoreType.DMA((19,)),
             pltpu.SemaphoreType.DMA((2, n_c)),
             pltpu.SemaphoreType.DMA((2,)),
         ],

time: 14.4 us -> 14.1 us (0.979)
  Pallas kernels: 14.2 us -> 13.9 us
    pallas_call x1, Pallas kernels: 11.5 us -> 11.2 us  [fast(): pl.pallas_call(functools.partial(send_kernel, (n_c, n_s, n_t, shard_rows)...]
where the time goes in v3:
time: 14.1 us; the launch traced here: 13.9 us
  Pallas kernels  13.9 us (99%)
    pallas_call x1, Pallas kernels, fast(): pl.pallas_call(functools.partial(send_kernel, (n_c, n_s, n_t, shard_rows)...  11.2 us
    pallas_call x1, Pallas kernels, fast(): pl.pallas_call(write_kernel, out_shape=jax.ShapeDtypeStruct((tokens, widt...  2.7 us

profile of v3, /device:TPU:5, one launch (start us, length us, event | category | flops | bytes accessed | tf_op | source)
XLA Modules:
  0.0 13.9 jit_solution(15802305399032050322)
XLA Ops:
  0.0 0.0 copy-start
  0.0 11.2 %send.1 = (bf16[512,128]{1,0:T(8,128)(2,1)S(1)}, bf16[128,5120]{1,0:T(8,128)(2,1)S(1)}, f32[512,5120]{1,0:T(8,128)S(1)}, f32[512,128]{1,0:T(8,128)S(1)}) custom-call(bf16[2,128,8,384]{3,2,1,0:T(8,128)(2,1)} %x_hbm.1, bf16[864,384]{1,0:T(8,128)(2,1)} %bitcast.10, f32[384]{0:T(512)} %gain_hbm.1, f32[16,32]{1,0:T(8,128)} %bitcast.15, f32[1,32]{1,0:T(1,128)} %bitcast.16, ...), custom_call_target="tpu_custom_call" | custom-call | tf_op jit(solution)/shard_map/send/pallas_call | solution.py:918
  11.2 0.0 copy-done
  11.2 2.7 %write.1 = bf16[512,5120]{1,0:T(8,128)(2,1)} custom-call(bf16[512,128]{1,0:T(8,128)(2,1)S(1)} %get-tuple-element.9.lhs, bf16[128,5120]{1,0:T(8,128)(2,1)S(1)} %get-tuple-element.10.late, f32[512,5120]{1,0:T(8,128)S(1)} %get-tuple-element.11.early, f32[512,128]{1,0:T(8,128)S(1)} %get-tuple-element.12.inv, f32[1,5120]{1,0:T(1,128)S(1)} %bitcast.9), custom_call_target="tpu_custom_call" | custom-call | tf_op jit(solution)/shard_map/write/pallas_call | solution.py:965
Async XLA Ops:
  0.0 11.2 %copy-start = (f32[5120]{0:T(1024)S(1)}, f32[5120]{0:T(1024)}, u32[]{:S(2)}) copy-start(f32[5120]{0:T(1024)} %param.26) | copy-start | bytes 61444

commit v4 on v3

--- a/solution.py
+++ b/solution.py
@@ -472,9 +472,9 @@
 
 def send_kernel(
     sizes, x_hbm, cw_hbm, gain_hbm, mw_hbm, cb_hbm, mb_hbm, noisy_hbm, mask_hbm, pw_hbm, xw_hbm, pb_hbm,
-    xb_hbm, scale_hbm, lhs_ref, late_ref, early_ref, inv_ref,
+    xb_hbm, scale_hbm, lhs_ref, late_ref, early_ref, own_gram, base,
     cwt, gain_ref, mw_ref, cb_ref, mb_ref, pb_ref, xb_ref, scale_ref, wt, xin, actf, cen, edge, msg, got,
-    lat_w, both, own, gram, own_gram, order, swap, bias_row, center, late_mean, x_early, base, in_sem, s_sem, r_sem,
+    lat_w, both, own, gram, order, swap, bias_row, center, late_mean, x_early, in_sem, s_sem, r_sem,
 ):
     n_c, n_s, n_t, shard_rows = sizes
     c, s, t = lax.axis_index("cfg"), lax.axis_index("seq"), lax.axis_index("tile")
@@ -495,31 +495,20 @@
     cut = half // 2 + 2
     start = c * (half - 1)
     xs = [
-        [
-            pltpu.make_async_copy(
-                x_hbm.at[f, pl.ds(start + lo, size)],
-                xin.at[f, pl.ds(1 - c + lo, size)],
-                in_sem.at[i * frames + f],
-            )
-            for f in range(frames)
-        ]
+        pltpu.make_async_copy(
+            x_hbm.at[:, pl.ds(start + lo, size)], xin.at[:, pl.ds(1 - c + lo, size)], in_sem.at[i]
+        )
         for i, (lo, size) in enumerate(((0, cut), (cut, half + 1 - cut)))
     ]
-    third = cw_hbm.shape[0] // K
-    taps = [
-        pltpu.make_async_copy(
-            cw_hbm.at[a * third : (a + 1) * third], cwt.at[a * third : (a + 1) * third], in_sem.at[4 + a]
-        )
-        for a in range(K)
-    ]
+    taps = pltpu.make_async_copy(cw_hbm, cwt, in_sem.at[2])
     small = [
-        pltpu.make_async_copy(src, dst, in_sem.at[7 + i])
+        pltpu.make_async_copy(src, dst, in_sem.at[3 + i])
         for i, (src, dst) in enumerate(
             ((gain_hbm, gain_ref), (mw_hbm, mw_ref), (cb_hbm, cb_ref), (mb_hbm, mb_ref))
         )
     ]
     later = [
-        pltpu.make_async_copy(src, dst, in_sem.at[11 + i])
+        pltpu.make_async_copy(src, dst, in_sem.at[i])
         for i, (src, dst) in enumerate(
             (
                 (pb_hbm, pb_ref), (xb_hbm, xb_ref), (scale_hbm, scale_ref), (noisy_hbm, own),
@@ -529,13 +518,10 @@
         )
     ]
     small[1].start()
-    for load in taps:
-        load.start()
-    for load in xs[0]:
-        load.start()
+    taps.start()
+    xs[0].start()
     small[0].start()
-    for load in xs[1]:
-        load.start()
+    xs[1].start()
     small[2].start()
     small[3].start()
 
@@ -592,17 +578,13 @@
 
     def convolve(m):
         lo = m * count
+        total = None
         for f in range(frames):
             taps = [actf[f, lo + b * columns : lo + b * columns + count, :].astype(BF16) for b in range(K)]
-            total = nt(jnp.concatenate(taps, axis=1), wt[:, f * K * channels : (f + 1) * K * channels])
-            cen[f, lo : lo + count, :] = total[:, :128]
-            edge[f, lo : lo + count, :] = total[:, 128:]
-
-    def both_frames(ref, at):
-        v = ref[0, pl.ds(at, 8, stride=2 * columns), :]
-        for f in range(1, frames):
-            v = v + ref[f, pl.ds(at, 8, stride=2 * columns), :]
-        return v
+            term = nt(jnp.concatenate(taps, axis=1), wt[:, f * K * channels : (f + 1) * K * channels])
+            total = term if total is None else total + jnp.maximum(term, -3e38)
+        cen[lo : lo + count, :] = total[:, :128]
+        edge[lo : lo + count, :] = total[:, 128:]
 
     lane = lax.broadcasted_iota(jnp.int32, (8, 128), 1)
     upper = lane >= 64
@@ -615,8 +597,8 @@
             mids, rights, lefts = [], [], []
             for w in range(columns):
                 starts = [((m * shard_rows + h * 8) * 2 + a) * columns + w for h in range(2)]
-                c0, c1 = (both_frames(cen, at) for at in starts)
-                e0, e1 = (both_frames(edge, at) for at in starts)
+                c0, c1 = (cen[pl.ds(at, 8, stride=2 * columns), :] for at in starts)
+                e0, e1 = (edge[pl.ds(at, 8, stride=2 * columns), :] for at in starts)
                 mids.append(jnp.where(upper, pltpu.roll(c1, 64, 1), c0))
                 turned = pltpu.roll(jnp.where(upper, e0, e1), 64, 1)
                 rights.append(jnp.where(upper, turned, e0))
@@ -684,29 +666,25 @@
     with jax.named_scope("loadt"):
         small[1].wait()
         parts = fold_parts(mw_ref)
-        for load in taps:
-            load.wait()
+        taps.wait()
     with jax.named_scope("fold"):
         fold_taps(cwt, parts, wt, z, range(K))
     with jax.named_scope("loadx"):
         small[0].wait()
-        for load in xs[0]:
-            load.wait()
+        xs[0].wait()
     with jax.named_scope("act0"):
         gain = gain_ref[...].reshape(1, channels) * (0.5 * channels**0.5)
-        activate(0, half // 2 + 2)
+        xs[1].wait()
+        small[2].wait()
+        small[3].wait()
         for load in later:
             load.start()
-    with jax.named_scope("conv0"):
+        activate(0, half // 2 + 2)
+        activate(half // 2 + 2, half + 2)
         convolve(0)
         pack(0)
-    with jax.named_scope("load1"):
-        small[2].wait()
-        small[3].wait()
-        for load in xs[1]:
-            load.wait()
-    ahead = (s < 2).astype(jnp.int32) + ((s == 0) & (t == 0)).astype(jnp.int32)
-    after = (ahead > 0).astype(jnp.int32)
+
+    after = (s < 2).astype(jnp.int32)
     block = 128
 
     @pl.loop(0, 2)
@@ -721,7 +699,6 @@
         @pl.when(turn == 0)
         def _():
             with jax.named_scope("conv1"):
-                activate(half // 2 + 2, half + 2)
                 convolve(1)
                 pack(1)
 
@@ -730,7 +707,7 @@
             with jax.named_scope("send1"):
                 send(1)
 
-        @pl.when(turn == (ahead == 0).astype(jnp.int32))
+        @pl.when(turn == 1 - after)
         def _():
             with jax.named_scope("loadw"):
                 for load in later:
@@ -764,7 +741,7 @@
                 noise = own[...].astype(F32).T
                 x_early[:, : 2 * split] = jnp.concatenate([noise, jnp.zeros_like(noise)], axis=1).astype(BF16)
 
-        @pl.when(turn == (ahead < 2).astype(jnp.int32))
+        @pl.when(turn == 1)
         def _():
             with jax.named_scope("gram"):
                 for part in range(2):
@@ -862,33 +839,32 @@
         for h in range(2):
             lhs_ref[h * n : (h + 1) * n, :] = twice[h].astype(BF16)
 
-    with jax.named_scope("stats"):
-        for k in range(0, tokens, block):
-            at = slice(k, k + block)
-            x = lhs_ref[at, :]
-            y = jnp.dot(x, own_gram[...], preferred_element_type=F32) + base[1, at, :]
-            upper = lax.broadcasted_iota(jnp.int32, (block, 128), 1) >= split
-            power = jnp.sum(jnp.where(upper, x.astype(F32) * y, 0.0) + base[0, at, :], axis=-1, keepdims=True)
-            variance = jnp.maximum(power * (1.0 / width), 0.0)
-            inv_ref[at, :] = jnp.broadcast_to(lax.rsqrt(variance + 1e-06), (block, 128))
-
-
-def write_kernel(lhs, late, early, inv, shift, out, buf, sem):
-    width = buf.shape[1]
-    wide = 512 if width % 512 == 0 else width
-    step = min(wide, 256)
-    copies = []
-    for k in range(0, width, wide):
-        for q in range(k, k + wide, step):
-            at = slice(q, q + step)
-            part = jnp.dot(lhs[...], late[:, at], preferred_element_type=F32)
-            factor = jnp.concatenate([inv[...]] * (step // 128), axis=1)
-            buf[:, at] = ((part + early[:, at]) * factor + shift[:, at]).astype(BF16)
-        copy = pltpu.make_async_copy(buf.at[:, k : k + wide], out.at[:, k : k + wide], sem.at[k // wide])
-        copy.start()
-        copies.append(copy)
-    for copy in copies:
-        copy.wait()
+
+def write_kernel(lhs, late, early, own_gram, base, shift, out, buf, inv, sem):
+    tokens, width = buf.shape
+    split = lhs.shape[1] // 2
+    block = 128
+    upper = lax.broadcasted_iota(jnp.int32, (block, 128), 1) >= split
+    for k in range(0, tokens, block):
+        at = slice(k, k + block)
+        x = lhs[at, :]
+        y = jnp.dot(x, own_gram[...], preferred_element_type=F32) + base[1, at, :]
+        power = jnp.sum(jnp.where(upper, x.astype(F32) * y, 0.0) + base[0, at, :], axis=-1, keepdims=True)
+        variance = jnp.maximum(power * (1.0 / width), 0.0)
+        inv[at, :] = jnp.broadcast_to(lax.rsqrt(variance + 1e-06), (block, 128))
+    step = 256 if width % 256 == 0 else width
+    steps = width // step
+    last = 0
+    for q in range(steps):
+        at = slice(q * step, (q + 1) * step)
+        part = jnp.dot(lhs[...], late[:, at], preferred_element_type=F32)
+        factor = jnp.concatenate([inv[...]] * (step // 128), axis=1)
+        buf[:, at] = ((part + early[:, at]) * factor + shift[:, at]).astype(BF16)
+        if q % 2 == 1 or q == steps - 1:
+            done = slice(last * step, (q + 1) * step)
+            pltpu.make_async_copy(buf.at[:, done], out.at[:, done], sem).start()
+            last = q + 1
+    pltpu.make_async_copy(buf, out, sem).wait()
 
 
 def fast(
@@ -921,10 +897,11 @@
             pltpu.VMEM((tokens, 2 * split), BF16),
             pltpu.VMEM((2 * split, width), BF16),
             pltpu.VMEM((tokens, width), F32),
-            pltpu.VMEM((tokens, 128), F32),
+            pltpu.VMEM((2 * split, 2 * split), BF16),
+            pltpu.VMEM((2, tokens, 128), F32),
         ),
         in_specs=[hbm] * len(args),
-        out_specs=(vmem,) * 4,
+        out_specs=(vmem,) * 5,
         scratch_shapes=[
             pltpu.VMEM(conv_weight.shape[::-1], BF16),
             pltpu.VMEM((channels,), F32),
@@ -937,23 +914,21 @@
             pltpu.VMEM((16 * z, frames * K * channels), BF16),
             pltpu.VMEM((frames, half + 2, columns, channels), BF16),
             pltpu.VMEM((frames, (half + 2) * columns, channels), F32),
-            pltpu.VMEM((frames, count, 128), F32),
-            pltpu.VMEM((frames, count, 128), F32),
+            pltpu.VMEM((count, 128), F32),
+            pltpu.VMEM((count, 128), F32),
             pltpu.VMEM((reach * chunks, per, 128), BF16),
             pltpu.VMEM((2, n_s, per, 128), BF16),
             pltpu.VMEM((split, width), BF16),
             pltpu.VMEM((depth + 16, width), BF16),
             pltpu.VMEM(noisy_tokens.shape[::-1], BF16),
             pltpu.VMEM((2, split + 16, depth), F32),
-            pltpu.VMEM((2 * split, 2 * split), BF16),
             pltpu.VMEM((n, n), BF16),
             pltpu.VMEM((split, split), BF16),
             pltpu.VMEM((1, 128), F32),
             pltpu.VMEM((1, width), F32),
             pltpu.VMEM((split, 128), F32),
             pltpu.VMEM((tokens, depth), BF16),
-            pltpu.VMEM((2, tokens, 128), F32),
-            pltpu.SemaphoreType.DMA((19,)),
+            pltpu.SemaphoreType.DMA((8,)),
             pltpu.SemaphoreType.DMA((2, n_c)),
             pltpu.SemaphoreType.DMA((2,)),
         ],
@@ -965,9 +940,9 @@
     return pl.pallas_call(
         write_kernel,
         out_shape=jax.ShapeDtypeStruct((tokens, width), BF16),
-        in_specs=[vmem] * 5,
+        in_specs=[vmem] * 6,
         out_specs=hbm,
-        scratch_shapes=[pltpu.VMEM((tokens, width), BF16), pltpu.SemaphoreType.DMA((max(1, width // 512),))],
+        scratch_shapes=[pltpu.VMEM((tokens, width), BF16), pltpu.VMEM((tokens, 128), F32), pltpu.SemaphoreType.DMA],
         compiler_params=pltpu.CompilerParams(vmem_limit_bytes=24 * 2**20),
         name="write",
     )(*prepared, norm_shift[None])

time: 14.1 us -> 13.8 us (0.979)
  Pallas kernels: 13.9 us -> 13.6 us
    pallas_call x1, Pallas kernels: 11.2 us -> 10.8 us  [fast(): pl.pallas_call(functools.partial(send_kernel, (n_c, n_s, n_t, shard_rows)...]
where the time goes in v4:
time: 13.8 us; the launch traced here: 13.6 us
  Pallas kernels  13.6 us (99%)
    pallas_call x1, Pallas kernels, fast(): pl.pallas_call(functools.partial(send_kernel, (n_c, n_s, n_t, shard_rows)...  10.8 us
    pallas_call x1, Pallas kernels, fast(): pl.pallas_call(write_kernel, out_shape=jax.ShapeDtypeStruct((tokens, widt...  2.75 us

profile of v4, /device:TPU:5, one launch (start us, length us, event | category | flops | bytes accessed | tf_op | source)
XLA Modules:
  0.0 13.6 jit_solution(7179873122105273366)
XLA Ops:
  0.0 0.0 copy-start
  0.0 10.8 %send.1 = (bf16[512,128]{1,0:T(8,128)(2,1)S(1)}, bf16[128,5120]{1,0:T(8,128)(2,1)S(1)}, f32[512,5120]{1,0:T(8,128)S(1)}, bf16[128,128]{1,0:T(8,128)(2,1)S(1)}, f32[2,512,128]{2,1,0:T(8,128)S(1)}) custom-call(bf16[2,128,8,384]{3,2,1,0:T(8,128)(2,1)} %x_hbm.1, bf16[864,384]{1,0:T(8,128)(2,1)} %bitcast.10, f32[384]{0:T(512)} %gain_hbm.1, f32[16,32]{1,0:T(8,128)} %bitcast.15, ...), custom_call_target="tpu_custom_call" | custom-call | tf_op jit(solution)/shard_map/send/pallas_call | solution.py:894
  10.8 0.0 copy-done
  10.9 2.7 %write.1 = bf16[512,5120]{1,0:T(8,128)(2,1)} custom-call(bf16[512,128]{1,0:T(8,128)(2,1)S(1)} %get-tuple-element.10.lhs, bf16[128,5120]{1,0:T(8,128)(2,1)S(1)} %get-tuple-element.11.late, f32[512,5120]{1,0:T(8,128)S(1)} %get-tuple-element.12.early, bf16[128,128]{1,0:T(8,128)(2,1)S(1)} %get-tuple-element.13.own_gram, ...), custom_call_target="tpu_custom_call" | custom-call | tf_op jit(solution)/shard_map/write/pallas_call | solution.py:940
Async XLA Ops:
  0.0 10.8 %copy-start = (f32[5120]{0:T(1024)S(1)}, f32[5120]{0:T(1024)}, u32[]{:S(2)}) copy-start(f32[5120]{0:T(1024)} %param.26) | copy-start | bytes 61444
